TPU v7x, 256 devices: a whole 4x4x8 slice. The times are simulated.
256 devices in a mesh: dp: 32 (over y, x, core), mp: 8 (over z).
Axes of the slice: x: 4, y: 4, z: 8, core: 2. Of those that a mesh axis runs over, the one named last changes fastest.
Arguments:
- users_list: int32 [256, 256], P(('dp', 'mp')), may hold values from 0 to 4095, as said below
- items_list: int32 [256, 256], P(('dp', 'mp')), may hold values from 0 to 4095, as said below
- days_list: int32 [256, 32], P(('dp', 'mp')), may hold values from 0 to 1023, as said below
- status: int32 [256, 32, 256, 256], P(('dp', 'mp')), may hold values from 0 to 2
- user_factor: float32 [4096, 256], P('dp', 'mp'), may hold values from -2.4 to 2.4
- user_first: float32 [4096, 256], P('dp', 'mp'), may hold values from -6 to 6
- user_second: float32 [4096, 256], P('dp', 'mp'), may hold values from 0.05 to 2
- item_factor: float32 [4096, 256], P('dp', 'mp'), may hold values from -2.4 to 2.4
- item_first: float32 [4096, 256], P('dp', 'mp'), may hold values from -6 to 6
- item_second: float32 [4096, 256], P('dp', 'mp'), may hold values from 0.05 to 2
- day_factor: float32 [1024, 256], P('dp', 'mp'), may hold values from -2.4 to 2.4
- day_first: float32 [1024, 256], P('dp', 'mp'), may hold values from -6 to 6
- day_second: float32 [1024, 256], P('dp', 'mp'), may hold values from 1 to 3000
Outputs:
- new_user_factor: float32 [4096, 256], P('dp', 'mp')
- new_user_first: float32 [4096, 256], P('dp', 'mp')
- new_user_second: float32 [4096, 256], P('dp', 'mp')
- new_item_factor: float32 [4096, 256], P('dp', 'mp')
- new_item_first: float32 [4096, 256], P('dp', 'mp')
- new_item_second: float32 [4096, 256], P('dp', 'mp')
- new_day_factor: float32 [1024, 256], P('dp', 'mp')
- new_day_first: float32 [1024, 256], P('dp', 'mp')
- new_day_second: float32 [1024, 256], P('dp', 'mp')
Inputs may be any that keep to these rules, and one draw needn't show every extreme that they name: `users_list`: the 256 users of a block are distinct; at most 12 of them lie in the rows n * 128 to (n + 1) * 128 - 1 of one index n of dp, and one such index holds exactly 12 users of every block. `items_list`: the 256 items of a block are distinct; at most 12 of them lie in the rows n * 128 to (n + 1) * 128 - 1 of one index n of dp, and one such index holds exactly 12 items of every block. `days_list`: the 32 days of a block are distinct; at most 2 of them lie in the rows n * 32 to (n + 1) * 32 - 1 of one index n of dp, and one such index holds exactly 2 days of every block.
All inputs are finite; a program needn't handle non-finite values.
Results may differ from a plain program's by a relative error of at most 0.0044.
Values may be sent and summed in bfloat16 or wider, within the bound.
A program may use at most 64 MiB of HBM per device.

v0:
```python
import jax
import jax.numpy as jnp
from jax import lax
from jax.sharding import PartitionSpec as P

beta_one = 0.9
beta_two = 0.99
bias_one = 1.0 - 0.9**10
bias_two = 1.0 - 0.99**10
learn_rate = 0.01
epsilon = 1e-08
loss_scale = 0.0625
zero_weight = 2.0


def block_grads(user_row_values, item_row_values, day_row_values, block_status):
    day_count = day_row_values.shape[0]
    user_count = user_row_values.shape[0]
    scaled = day_row_values[:, None, :] * user_row_values[None, :, :]
    scaled_flat = scaled.reshape(day_count * user_count, -1)
    logits = jnp.einsum(
        "nr,ir->ni", scaled_flat, item_row_values, preferred_element_type=jnp.float32
    )
    chance = jax.nn.sigmoid(logits)
    status_flat = block_status.reshape(day_count * user_count, -1)
    residual = loss_scale * (
        jnp.where(status_flat == 1, chance - 1.0, 0.0)
        + jnp.where(status_flat == 2, zero_weight * chance, 0.0)
    )
    residual = residual.astype(jnp.bfloat16)
    projected = jnp.dot(residual, item_row_values, preferred_element_type=jnp.float32).reshape(
        day_count, user_count, -1
    )
    user_gradient = jnp.sum(projected * day_row_values[:, None, :].astype(jnp.float32), axis=0)
    day_gradient = jnp.sum(projected * user_row_values[None, :, :].astype(jnp.float32), axis=1)
    item_gradient = jnp.einsum(
        "ni,nr->ir", residual, scaled_flat, preferred_element_type=jnp.float32
    )
    return (user_gradient, item_gradient, day_gradient)


def adam_update(factor, first, second, gradient):
    first_new = beta_one * first + (1.0 - beta_one) * gradient
    second_new = beta_two * second + (1.0 - beta_two) * gradient * gradient
    change = learn_rate * (first_new / bias_one) / (jnp.sqrt(second_new / bias_two) + epsilon)
    return (factor - change, first_new, second_new)


def slot_layout(wanted_row_list, locally_kept_lines, line_bundles):
    holder_index = wanted_row_list // locally_kept_lines
    local_row = wanted_row_list % locally_kept_lines
    onehot = (
        holder_index[:, :, None] == jnp.arange(line_bundles, dtype=jnp.int32)[None, None, :]
    ).astype(jnp.int32)
    before = jnp.cumsum(onehot, axis=1) - onehot
    slot_position_index = jnp.sum(before * onehot, axis=2)
    return (holder_index, local_row, slot_position_index)


def build_needed_catalogs(desired_line_catalogs, locally_kept_counts, place_limits, line_bundles):
    buffers = []
    for wanted_row_list, locally_kept_lines, place_limit in zip(
        desired_line_catalogs, locally_kept_counts, place_limits
    ):
        holder_index, local_row, slot_position_index = slot_layout(
            wanted_row_list, locally_kept_lines, line_bundles
        )
        blocks = jnp.broadcast_to(
            jnp.arange(wanted_row_list.shape[0], dtype=jnp.int32)[:, None], wanted_row_list.shape
        )
        blank_slots = jnp.full((line_bundles, wanted_row_list.shape[0], place_limit), -1, jnp.int32)
        buffers.append(blank_slots.at[holder_index, blocks, slot_position_index].set(local_row))
    return jnp.concatenate(buffers, axis=2)


def collect_needed_lines(desired_line_catalogs, locally_kept_counts, place_limits, line_bundles):
    return lax.all_to_all(
        build_needed_catalogs(
            desired_line_catalogs, locally_kept_counts, place_limits, line_bundles
        ),
        "dp",
        split_axis=0,
        concat_axis=0,
        tiled=True,
    )


def serve_needed_lines(needed_line_numbers, loading_tables, place_limits):
    pieces = []
    offset = 0
    for loading_table, place_limit in zip(loading_tables, place_limits):
        wanted = needed_line_numbers[:, :, offset : offset + place_limit]
        taken_rows = jnp.take(
            loading_table, jnp.clip(wanted, 0, loading_table.shape[0] - 1), axis=0
        )
        pieces.append(
            jnp.where((wanted >= 0)[..., None], taken_rows, jnp.zeros((), loading_table.dtype))
        )
        offset = offset + place_limit
    return jnp.concatenate(pieces, axis=2)


def slot_targets(place_layout, place_limit):
    holder_index, slot_position_index = place_layout
    return holder_index[0] * place_limit + slot_position_index[0]


def pick_lines(arrived_lines, place_layouts, place_limits, line_bundles):
    picked = []
    offset = 0
    for place_layout, place_limit in zip(place_layouts, place_limits):
        flat_slots = arrived_lines[:, 0, offset : offset + place_limit, :].reshape(
            line_bundles * place_limit, -1
        )
        target = slot_targets(place_layout, place_limit)
        selector = (
            target[:, None] == jnp.arange(line_bundles * place_limit, dtype=jnp.int32)[None, :]
        ).astype(jnp.bfloat16)
        picked.append(
            jnp.dot(selector, flat_slots, preferred_element_type=jnp.float32).astype(jnp.bfloat16)
        )
        offset = offset + place_limit
    return picked


def derivative_place_numbers(slope_numbers, place_layouts, place_limits, line_bundles):
    pieces = []
    for row_gradient, place_layout, place_limit in zip(slope_numbers, place_layouts, place_limits):
        target = slot_targets(place_layout, place_limit)
        placer = (
            jnp.arange(line_bundles * place_limit, dtype=jnp.int32)[:, None] == target[None, :]
        ).astype(jnp.float32)
        placed = jnp.dot(
            placer,
            row_gradient,
            precision=lax.Precision.HIGHEST,
            preferred_element_type=jnp.float32,
        )
        pieces.append(placed.reshape(line_bundles, place_limit, -1))
    return jnp.concatenate(pieces, axis=1)[:, None, :, :]


def keeper_slope_totals(arrived_lines, needed_line_numbers, locally_kept_counts, place_limits):
    totals = []
    offset = 0
    for locally_kept_lines, place_limit in zip(locally_kept_counts, place_limits):
        wanted = needed_line_numbers[:, :, offset : offset + place_limit].reshape(-1)
        values = arrived_lines[:, :, offset : offset + place_limit, :].reshape(wanted.shape[0], -1)
        onehot = (
            jnp.arange(locally_kept_lines, dtype=jnp.int32)[:, None] == wanted[None, :]
        ).astype(jnp.float32)
        totals.append(
            jnp.dot(
                onehot, values, precision=lax.Precision.HIGHEST, preferred_element_type=jnp.float32
            )
        )
        offset = offset + place_limit
    return totals


def local(
    users_list,
    items_list,
    days_list,
    status,
    user_factor,
    user_first,
    user_second,
    item_factor,
    item_first,
    item_second,
    day_factor,
    day_first,
    day_second,
):
    line_bundles = lax.axis_size("dp")
    place_limits = (
        max(2, 3 * users_list.shape[1] // (2 * line_bundles)),
        max(2, 3 * items_list.shape[1] // (2 * line_bundles)),
        max(2, 2 * days_list.shape[1] // line_bundles),
    )
    locally_kept_counts = (user_factor.shape[0], item_factor.shape[0], day_factor.shape[0])
    loading_tables = (
        user_factor.astype(jnp.bfloat16),
        item_factor.astype(jnp.bfloat16),
        day_factor.astype(jnp.bfloat16),
    )
    own_lists = (users_list, items_list, days_list)
    place_layouts = []
    for wanted_row_list, locally_kept_lines in zip(own_lists, locally_kept_counts):
        holder_index, local_row, slot_position_index = slot_layout(
            wanted_row_list, locally_kept_lines, line_bundles
        )
        place_layouts.append((holder_index, slot_position_index))
    bundled_line_catalogs = (
        lax.all_gather(users_list, "mp", axis=0, tiled=True),
        lax.all_gather(items_list, "mp", axis=0, tiled=True),
        lax.all_gather(days_list, "mp", axis=0, tiled=True),
    )
    needed_line_numbers = collect_needed_lines(
        bundled_line_catalogs, locally_kept_counts, place_limits, line_bundles
    )
    served_lines = serve_needed_lines(needed_line_numbers, loading_tables, place_limits)
    arrived_lines = lax.all_to_all(
        lax.all_to_all(served_lines, "dp", split_axis=0, concat_axis=0, tiled=True),
        "mp",
        split_axis=1,
        concat_axis=3,
        tiled=True,
    )
    user_row_values, item_row_values, day_row_values = pick_lines(
        arrived_lines, place_layouts, place_limits, line_bundles
    )
    user_gradient, item_gradient, day_gradient = block_grads(
        user_row_values, item_row_values, day_row_values, status[0]
    )
    slot_storage = derivative_place_numbers(
        (user_gradient, item_gradient, day_gradient), place_layouts, place_limits, line_bundles
    )
    returned_lines = lax.all_to_all(
        lax.all_to_all(
            slot_storage.astype(jnp.bfloat16), "dp", split_axis=0, concat_axis=0, tiled=True
        ),
        "mp",
        split_axis=3,
        concat_axis=1,
        tiled=True,
    ).astype(slot_storage.dtype)
    user_gradient_sum, item_gradient_sum, day_gradient_sum = keeper_slope_totals(
        returned_lines, needed_line_numbers, locally_kept_counts, place_limits
    )
    new_user_factor, new_user_first, new_user_second = adam_update(
        user_factor, user_first, user_second, user_gradient_sum
    )
    new_item_factor, new_item_first, new_item_second = adam_update(
        item_factor, item_first, item_second, item_gradient_sum
    )
    new_day_factor, new_day_first, new_day_second = adam_update(
        day_factor, day_first, day_second, day_gradient_sum
    )
    return (
        new_user_factor,
        new_user_first,
        new_user_second,
        new_item_factor,
        new_item_first,
        new_item_second,
        new_day_factor,
        new_day_first,
        new_day_second,
    )


def solution(mesh):
    placed = (
        P(("dp", "mp"), None),
        P(("dp", "mp"), None),
        P(("dp", "mp"), None),
        P(("dp", "mp"), None, None, None),
        P("dp", "mp"),
        P("dp", "mp"),
        P("dp", "mp"),
        P("dp", "mp"),
        P("dp", "mp"),
        P("dp", "mp"),
        P("dp", "mp"),
        P("dp", "mp"),
        P("dp", "mp"),
    )
    return jax.shard_map(
        local,
        mesh=mesh,
        in_specs=placed,
        out_specs=(
            P("dp", "mp"),
            P("dp", "mp"),
            P("dp", "mp"),
            P("dp", "mp"),
            P("dp", "mp"),
            P("dp", "mp"),
            P("dp", "mp"),
            P("dp", "mp"),
            P("dp", "mp"),
        ),
        check_vma=False,
    )
```

profile of v0, /device:TPU:1, one launch (start us, length us, event | category | flops | bytes accessed | tf_op | source)
XLA Modules:
  0.0 253.2 jit_solution(11304306322711976860)
XLA Ops:
  0.7 16.3 %all-gather.2 = s32[8,1,32]{2,1,0:T(1,128)S(1)} all-gather(s32[1,1,32]{2,1,0:T(1,128)} %bitcast.310), channel_id=1, replica_groups=mesh['dp'=32,'mp'=8] {'mp'}, dimensions={0}, use_global_device_ids=true | all-gather | bytes 1152 | tf_op jit(solution)/shard_map/all_gather | solution.py:198
  16.9 10.1 %all-gather.1 = s32[8,1,256]{2,1,0:T(1,128)S(1)} all-gather(s32[1,1,256]{2,1,0:T(1,128)} %bitcast.300), channel_id=1, replica_groups=mesh['dp'=32,'mp'=8] {'mp'}, dimensions={0}, use_global_device_ids=true | all-gather | bytes 9216 | tf_op jit(solution)/shard_map/all_gather | solution.py:197
  27.1 11.7 %all-gather = s32[8,1,256]{2,1,0:T(1,128)S(1)} all-gather(s32[1,1,256]{2,1,0:T(1,128)} %bitcast.301), channel_id=1, replica_groups=mesh['dp'=32,'mp'=8] {'mp'}, dimensions={0}, use_global_device_ids=true | all-gather | bytes 9216 | tf_op jit(solution)/shard_map/all_gather | solution.py:196
  40.1 4.6 %reduce-window.30 = s32[8,32,2,128]{3,1,2,0:T(8,128)S(1)} reduce-window(s32[8,32,2,128]{3,1,2,0:T(8,128)S(1)} %fusion.19, s32[]{:T(128)} %constant.178.clone.1), window={size=1x1x1x128 pad=0_0x0_0x0_0x127_0}, to_apply=%region_4.5 | reduce-window | flops 8323072 | bytes 524292 | tf_op jit(solution)/shard_map/reduce-window.2
  44.7 4.6 %reduce-window.26 = s32[8,32,2,128]{3,1,2,0:T(8,128)S(1)} reduce-window(s32[8,32,2,128]{3,1,2,0:T(8,128)S(1)} %fusion.18, s32[]{:T(128)} %constant.178.clone.1), window={size=1x1x1x128 pad=0_0x0_0x0_0x127_0}, to_apply=%region_0.1 | reduce-window | flops 8323072 | bytes 524292 | tf_op jit(solution)/shard_map/reduce-window
  50.7 8.1 %scatter_custom_fusion.1 = s32[3072]{0:T(1024)S(1)} fusion(s32[2048]{0:T(1024)S(1)} %bitcast.305, s32[2048]{0:T(1024)S(1)} %bitcast.302, s32[]{:T(128)} %constant.176.clone.1), kind=kCustom, calls=%fused_computation.181 | custom fusion | bytes 12292
  58.8 8.1 %scatter_custom_fusion.2 = s32[3072]{0:T(1024)S(1)} fusion(s32[2048]{0:T(1024)S(1)} %bitcast.304, s32[2048]{0:T(1024)S(1)} %bitcast.303, s32[]{:T(128)} %constant.176.clone.1), kind=kCustom, calls=%fused_computation.179 | custom fusion | bytes 12292
  67.0 15.1 %scatter_fusion = s32[32,8,2]{0,1,2:T(8,128)S(1)} fusion(s32[32,8,2]{0,1,2:T(8,128)S(1)} %broadcast_in_dim.73, s32[256]{0:T(256)S(1)} %reshape.575, s32[256]{0:T(256)S(1)} %reshape.577), kind=kCustom, calls=%fused_computation.3 | custom fusion | bytes 6144 | tf_op jit(solution)/shard_map/scatter | solution.py:72
  83.0 18.8 %all-to-all-start = ((s32[32,1,208]{2,1,0:T(1,128)}), s32[32,1,208]{2,1,0:T(1,128)S(1)}, u32[]{:S(2)}, u32[]{:S(2)}) async-start(s32[32,1,208]{2,1,0:T(1,128)} %reshape.621), calls=%async_computation | async-start | bytes 65536 | tf_op jit(solution)/shard_map/all_to_all | solution.py:77
  112.1 9.2 %gather_fusion.2 = bf16[3072,32]{1,0:T(8,128)(2,1)S(1)} fusion(bf16[128,32]{1,0:T(8,128)(2,1)S(1)} %copy.223, s32[3072]{0:T(1024)S(1)} %broadcast_clamp_fusion), kind=kCustom, calls=%fused_computation.1.clone | custom fusion | bytes 405504 | tf_op jit(solution)/shard_map/jit(_take)/gather | solution.py:93
  121.5 9.2 %gather_fusion.1 = bf16[3072,32]{1,0:T(8,128)(2,1)S(1)} fusion(bf16[128,32]{1,0:T(8,128)(2,1)S(1)} %copy.222, s32[3072]{0:T(1024)S(1)} %broadcast_clamp_fusion.1), kind=kCustom, calls=%fused_computation.clone | custom fusion | bytes 405504 | tf_op jit(solution)/shard_map/jit(_take)/gather | solution.py:93
  139.6 6.6 %all-to-all-start.1 = ((bf16[32,2,3328]{2,1,0:T(2,128)(2,1)}), bf16[32,2,3328]{2,1,0:T(2,128)(2,1)S(1)}, u32[]{:S(2)}, u32[]{:S(2)}) async-start(bf16[32,2,3328]{2,1,0:T(2,128)(2,1)} %reshape.623), calls=%async_computation.1 | async-start | bytes 851968 | tf_op jit(solution)/shard_map/all_to_all | solution.py:205
  147.3 9.4 %all-to-all-done.1 = bf16[32,2,3328]{2,1,0:T(2,128)(2,1)S(1)} async-done(((bf16[32,2,3328]{2,1,0:T(2,128)(2,1)}), bf16[32,2,3328]{2,1,0:T(2,128)(2,1)S(1)}, u32[]{:S(2)}, u32[]{:S(2)}) %all-to-all-start.1) | async-done | bytes 426016 | tf_op jit(solution)/shard_map/all_to_all | solution.py:205
  160.3 3.7 %all-to-all-start.2 = ((bf16[8,2,13312]{2,1,0:T(2,128)(2,1)}), bf16[8,2,13312]{2,1,0:T(2,128)(2,1)S(1)}, u32[]{:S(2)}, u32[]{:S(2)}) async-start(bf16[8,2,13312]{2,1,0:T(2,128)(2,1)} %reshape.625), calls=%async_computation.2 | async-start | bytes 851968 | tf_op jit(solution)/shard_map/all_to_all | solution.py:204
  164.0 6.1 %broadcast_compare_fusion.1 = (pred[1,32,256,256]{3,2,1,0:T(32,128)(4,1)}, pred[1,32,256,256]{3,2,1,0:T(32,128)(4,1)}) fusion(s32[1,32,256,256]{3,2,1,0:T(8,128)} %param.18), kind=kLoop, calls=%fused_computation.14 | loop fusion | flops 4194304 | bytes 12582912 | tf_op jit(solution)/shard_map/eq | solution.py:27
  170.1 8.5 %all-to-all-done.2 = bf16[8,2,13312]{2,1,0:T(2,128)(2,1)S(1)} async-done(((bf16[8,2,13312]{2,1,0:T(2,128)(2,1)}), bf16[8,2,13312]{2,1,0:T(2,128)(2,1)S(1)}, u32[]{:S(2)}, u32[]{:S(2)}) %all-to-all-start.2) | async-done | bytes 426016 | tf_op jit(solution)/shard_map/all_to_all | solution.py:204
  184.4 4.5 %multiply_convert_fusion = bf16[8192,256]{1,0:T(8,128)(2,1)S(1)} fusion(pred[1,32,256,256]{3,2,1,0:T(32,128)(4,1)S(1)} %copy-done.2, pred[1,32,256,256]{3,2,1,0:T(32,128)(4,1)S(1)} %copy-done.1, bf16[8192,256]{1,0:T(8,128)(2,1)S(1)} %bitcast.270, bf16[256,256]{1,0:T(8,128)(2,1)S(1)} %convolution_convert_fusion.2), kind=kOutput, calls=%fused_computation.12 | convolution fusion | flops 1094713344 | bytes 12713984 | tf_op jit(solution)/shard_map/nr,ir->ni/dot_general | solution.py:21
  191.3 3.5 %multiply_reduce_fusion = (f32[32,256]{1,0:T(8,128)S(1)}, f32[8192,256]{1,0:T(8,128)S(1)}) fusion(f32[256,256]{1,0:T(8,128)S(1)} %get-tuple-element.49, bf16[8192,256]{1,0:T(8,128)(2,1)} %copy-done, bf16[256,256]{1,0:T(8,128)(2,1)S(1)} %convolution_convert_fusion.2), kind=kOutput, calls=%fused_computation.10 | convolution fusion | flops 1077927936 | bytes 13008896 | tf_op jit(solution)/shard_map/dot_general | solution.py:31
  196.8 16.5 %all_to_all.51 = bf16[32,1,26,256]{3,2,1,0:T(8,128)(2,1)S(1)} all-to-all(bf16[32,1,26,256]{3,2,1,0:T(8,128)(2,1)S(1)} %copy.234), channel_id=1, replica_groups=mesh['dp'=32,'mp'=8] {'dp'}, dimensions={0} | all-to-all | bytes 851968 | tf_op jit(solution)/shard_map/all_to_all | solution.py:221
  213.3 3.2 %copy.235 = bf16[32,1,26,256]{0,2,1,3:T(8,128)(2,1)S(1)} copy(bf16[32,1,26,256]{3,2,1,0:T(8,128)(2,1)S(1)} %all_to_all.51) | data formatting | bytes 851968 | tf_op jit(solution)/shard_map/all_to_all | solution.py:221
  218.6 3.5 %all-to-all-start.4 = ((bf16[8,2,13312]{2,1,0:T(2,128)(2,1)}), bf16[8,2,13312]{2,1,0:T(2,128)(2,1)S(1)}, u32[]{:S(2)}, u32[]{:S(2)}) async-start(bf16[8,2,13312]{2,1,0:T(2,128)(2,1)} %reshape.627), calls=%async_computation.4 | async-start | bytes 851968 | tf_op jit(solution)/shard_map/all_to_all | solution.py:220
  222.4 15.4 %all-to-all-done.4 = bf16[8,2,13312]{2,1,0:T(2,128)(2,1)S(1)} async-done(((bf16[8,2,13312]{2,1,0:T(2,128)(2,1)}), bf16[8,2,13312]{2,1,0:T(2,128)(2,1)S(1)}, u32[]{:S(2)}, u32[]{:S(2)}) %all-to-all-start.4) | async-done | bytes 426016 | tf_op jit(solution)/shard_map/all_to_all | solution.py:220
  237.8 2.7 %reshape.628 = bf16[256,1,26,32]{3,2,1,0:T(8,128)(2,1)} reshape(bf16[8,2,13312]{2,1,0:T(2,128)(2,1)S(1)} %all-to-all-done.4) | data formatting | bytes 851968
  240.5 6.0 %copy.236 = bf16[32,1,26,8,32]{4,2,3,0,1:T(8,128)(2,1)S(1)} copy(bf16[32,1,26,8,32]{0,2,4,3,1:T(8,128)(2,1)} %bitcast.276) | data formatting | bytes 851968 | tf_op jit(solution)/shard_map/all_to_all | solution.py:220
  (201 shorter events, 46.3 us)
Async XLA Ops:
  0.6 49.8 %copy-start.22 = (s32[3]{0:T(128)S(1)}, s32[3]{0:T(128)}, u32[]{:S(2)}) copy-start(s32[3]{0:T(128)} %constant.207) | copy-start | bytes 40
  0.7 49.9 %copy-start.21 = (s32[3]{0:T(128)S(1)}, s32[3]{0:T(128)}, u32[]{:S(2)}) copy-start(s32[3]{0:T(128)} %constant.204) | copy-start | bytes 40
  67.0 34.9 %copy-start.24 = (s32[1,32]{1,0:T(1,128)S(1)}, s32[1,32]{1,0:T(1,128)}, u32[]{:S(2)}) copy-start(s32[1,32]{1,0:T(1,128)} %param.17) | copy-start | bytes 388
  67.0 34.9 %copy-start.14 = (s32[1,256]{1,0:T(1,128)S(1)}, s32[1,256]{1,0:T(1,128)}, u32[]{:S(2)}) copy-start(s32[1,256]{1,0:T(1,128)} %param.15) | copy-start | bytes 3076
  67.0 34.9 %copy-start.13 = (s32[1,256]{1,0:T(1,128)S(1)}, s32[1,256]{1,0:T(1,128)}, u32[]{:S(2)}) copy-start(s32[1,256]{1,0:T(1,128)} %param.16) | copy-start | bytes 3076
  67.0 41.0 %copy-start.11 = (f32[128,32]{0,1:T(8,128)S(1)}, f32[128,32]{0,1:T(8,128)}, u32[]{:S(2)}) copy-start(f32[128,32]{0,1:T(8,128)} %param.19) | copy-start | bytes 49156
  67.0 41.0 %copy-start.9 = (f32[128,32]{0,1:T(8,128)S(1)}, f32[128,32]{0,1:T(8,128)}, u32[]{:S(2)}) copy-start(f32[128,32]{0,1:T(8,128)} %param.22) | copy-start | bytes 49156
  67.0 41.0 %copy-start.5 = (f32[32,32]{1,0:T(8,128)S(1)}, f32[32,32]{1,0:T(8,128)}, u32[]{:S(2)}) copy-start(f32[32,32]{1,0:T(8,128)} %param.25) | copy-start | bytes 12292
  83.0 26.0 %all-to-all-start = ((s32[32,1,208]{2,1,0:T(1,128)}), s32[32,1,208]{2,1,0:T(1,128)S(1)}, u32[]{:S(2)}, u32[]{:S(2)}) async-start(s32[32,1,208]{2,1,0:T(1,128)} %reshape.621), calls=%async_computation | async-start | bytes 65536 | tf_op jit(solution)/shard_map/all_to_all | solution.py:77
  139.6 17.1 %all-to-all-start.1 = ((bf16[32,2,3328]{2,1,0:T(2,128)(2,1)}), bf16[32,2,3328]{2,1,0:T(2,128)(2,1)S(1)}, u32[]{:S(2)}, u32[]{:S(2)}) async-start(bf16[32,2,3328]{2,1,0:T(2,128)(2,1)} %reshape.623), calls=%async_computation.1 | async-start | bytes 851968 | tf_op jit(solution)/shard_map/all_to_all | solution.py:205
  160.3 18.3 %all-to-all-start.2 = ((bf16[8,2,13312]{2,1,0:T(2,128)(2,1)}), bf16[8,2,13312]{2,1,0:T(2,128)(2,1)S(1)}, u32[]{:S(2)}, u32[]{:S(2)}) async-start(bf16[8,2,13312]{2,1,0:T(2,128)(2,1)} %reshape.625), calls=%async_computation.2 | async-start | bytes 851968 | tf_op jit(solution)/shard_map/all_to_all | solution.py:204
  179.8 3.0 %copy-start.19 = (s32[256]{0:T(256)S(1)}, s32[256]{0:T(256)}, u32[]{:S(2)}) copy-start(s32[256]{0:T(256)} %multiply_add_fusion.6) | copy-start | bytes 3076
  179.8 3.3 %copy-start.16 = (s32[256]{0:T(256)S(1)}, s32[256]{0:T(256)}, u32[]{:S(2)}) copy-start(s32[256]{0:T(256)} %multiply_add_fusion.7) | copy-start | bytes 3076
  196.5 25.7 %copy-start.4 = (s32[32,8,12]{2,1,0:T(8,128)S(1)}, s32[32,8,12]{2,1,0:T(8,128)}, u32[]{:S(2)}) copy-start(s32[32,8,12]{2,1,0:T(8,128)} %get-tuple-element.35) | copy-start | bytes 36868
  196.5 25.8 %copy-start.3 = (s32[32,8,12]{2,1,0:T(8,128)S(1)}, s32[32,8,12]{2,1,0:T(8,128)}, u32[]{:S(2)}) copy-start(s32[32,8,12]{2,1,0:T(8,128)} %get-tuple-element.38) | copy-start | bytes 36868
  218.6 19.2 %all-to-all-start.4 = ((bf16[8,2,13312]{2,1,0:T(2,128)(2,1)}), bf16[8,2,13312]{2,1,0:T(2,128)(2,1)S(1)}, u32[]{:S(2)}, u32[]{:S(2)}) async-start(bf16[8,2,13312]{2,1,0:T(2,128)(2,1)} %reshape.627), calls=%async_computation.4 | async-start | bytes 851968 | tf_op jit(solution)/shard_map/all_to_all | solution.py:220
  246.5 3.6 %copy-start.7 = (f32[32,32]{1,0:T(8,128)S(1)}, f32[32,32]{1,0:T(8,128)}, u32[]{:S(2)}) copy-start(f32[32,32]{1,0:T(8,128)} %param.26) | copy-start | bytes 12292
  246.5 3.6 %copy-start.8 = (f32[32,32]{1,0:T(8,128)S(1)}, f32[32,32]{1,0:T(8,128)}, u32[]{:S(2)}) copy-start(f32[32,32]{1,0:T(8,128)} %param.27) | copy-start | bytes 12292
  246.6 4.4 %copy-start.10 = (f32[128,32]{0,1:T(8,128)S(1)}, f32[128,32]{0,1:T(8,128)}, u32[]{:S(2)}) copy-start(f32[128,32]{0,1:T(8,128)} %param.22) | copy-start | bytes 49156
  246.6 4.4 %copy-start.25 = (f32[128,32]{0,1:T(8,128)S(1)}, f32[128,32]{0,1:T(8,128)}, u32[]{:S(2)}) copy-start(f32[128,32]{0,1:T(8,128)} %param.23) | copy-start | bytes 49156
  246.6 4.3 %copy-start.26 = (f32[128,32]{0,1:T(8,128)S(1)}, f32[128,32]{0,1:T(8,128)}, u32[]{:S(2)}) copy-start(f32[128,32]{0,1:T(8,128)} %param.24) | copy-start | bytes 49156
  246.7 5.4 %copy-start.12 = (f32[128,32]{0,1:T(8,128)S(1)}, f32[128,32]{0,1:T(8,128)}, u32[]{:S(2)}) copy-start(f32[128,32]{0,1:T(8,128)} %param.19) | copy-start | bytes 49156
  246.7 5.3 %copy-start.27 = (f32[128,32]{0,1:T(8,128)S(1)}, f32[128,32]{0,1:T(8,128)}, u32[]{:S(2)}) copy-start(f32[128,32]{0,1:T(8,128)} %param.20) | copy-start | bytes 49156
  246.7 5.3 %copy-start.28 = (f32[128,32]{0,1:T(8,128)S(1)}, f32[128,32]{0,1:T(8,128)}, u32[]{:S(2)}) copy-start(f32[128,32]{0,1:T(8,128)} %param.21) | copy-start | bytes 49156
  (9 other events, 14.8 us)
where the time goes:
time: 254 us; the launch traced here: 253 us
  local copies, waits for them, and re-layouts  85.5 us (34%)
  blocking collectives  54.6 us (21%)
  waiting for transfers between devices  34.1 us (13%)
  starting transfers between devices  32.5 us (13%)
  other arithmetic  31 us (12%)
  matrix products  13.9 us (5%)
    unnamed x74, local copies, waits for them, and re-layouts  29.4 us
    gather x5, local copies, waits for them, and re-layouts, serve_needed_lines(): jnp.take(loading_table, jnp.clip(wanted, 0, loading_table.shape[0] - 1),...  20.1 us
    all_to_all x1, starting transfers between devices, collect_needed_lines(): lax.all_to_all(build_needed_catalogs(desired_line_catalogs, locally_kept_...  18.8 us
    all_to_all x1, blocking collectives, local(): lax.all_to_all(slot_storage.astype(jnp.bfloat16), 'dp', split_axis=0, con...  16.5 us
    all_gather x1, blocking collectives, local(): lax.all_gather(days_list, 'mp', axis=0, tiled=True)  16.3 us
    all_to_all x1, waiting for transfers between devices, local(): lax.all_to_all(lax.all_to_all(slot_storage.astype(jnp.bfloat16), 'dp', sp...  15.4 us
    scatter x1, local copies, waits for them, and re-layouts, build_needed_catalogs(): blank_slots.at[holder_index, blocks, slot_position_index].set(local_row)  15.1 us
    all_gather x1, blocking collectives, local(): lax.all_gather(users_list, 'mp', axis=0, tiled=True)  11.7 us
  transfers between devices with their start and end apart: 4, of which 4 were waited for; matrix products, arithmetic and copies ran while one was open for 5% of the time, Pallas kernels for 0%

commit v1 on v0

v1 whole, which is shorter than its diff:
```python
import functools

import jax
import jax.numpy as jnp
from jax import lax
from jax.experimental import pallas as pl
from jax.experimental.pallas import tpu as pltpu
from jax.sharding import PartitionSpec as P

MESH = pl.DeviceIdType.MESH
F32, BF16, I32 = jnp.float32, jnp.bfloat16, jnp.int32

beta_one = 0.9
beta_two = 0.99
bias_one = 1.0 - 0.9**10
bias_two = 1.0 - 0.99**10
learn_rate = 0.01
epsilon = 1e-08

SLOTS = 16
DAY_SLOT = 12
DAY_BASE = 128
ROWS = 384
CHUNKS = 4


def iota(shape, dim):
    return lax.broadcasted_iota(I32, shape, dim)


def onehot(hit):
    return jnp.where(hit, 1.0, 0.0).astype(BF16)


def dot(a, b):
    return jnp.dot(a, b, preferred_element_type=F32)


def dot_nt(a, b):
    return lax.dot_general(a, b, (((1,), (1,)), ((), ())), preferred_element_type=F32)


def list_layout(rows_wanted, per_owner, owners, base, first_slot):
    n = rows_wanted.shape[1]
    owner = rows_wanted // per_owner
    code = (rows_wanted - owner * per_owner + base + 1).astype(F32)
    hit = owner == iota((owners, n), 0)
    before = onehot(iota((n, n), 0) < iota((n, n), 1))
    rank = dot(onehot(hit), before)
    slot = jnp.sum(jnp.where(hit, rank, 0.0), axis=0, keepdims=True).astype(I32) + first_slot
    coded = jnp.where(hit, code, 0.0).astype(BF16)
    return coded, slot, owner * SLOTS


def step_kernel(
    owners,
    peers,
    users_ref,
    items_ref,
    days_ref,
    status_hbm,
    user_ref,
    item_ref,
    day_ref,
    grad_ref,
    status_ref,
    list_out,
    list_in,
    table,
    row_out,
    row_in,
    slope_out,
    slope_in,
    part_out,
    part_in,
    serve_ud,
    serve_it,
    user_rows,
    user_rows_t,
    item_rows,
    item_half,
    day_rows,
    user_acc,
    item_acc,
    day_acc,
    status_sem,
    send_sem,
    recv_sem,
):
    me_d = lax.axis_index("dp")
    me_m = lax.axis_index("mp")
    tall = owners * SLOTS
    days_here = status_ref.shape[0]
    per_chunk = days_here // CHUNKS

    def status_copy(chunk):
        part = pl.ds(chunk * per_chunk, per_chunk)
        return pltpu.make_async_copy(
            status_hbm.at[0, part], status_ref.at[part], status_sem.at[chunk]
        )

    for chunk in range(CHUNKS):
        status_copy(chunk).start()

    barrier = pltpu.get_barrier_semaphore()

    @pl.loop(1, owners)
    def _(delta):
        pl.semaphore_signal(
            barrier, inc=1, device_id=(lax.rem(me_d + delta, owners), me_m), device_id_type=MESH
        )

    @pl.loop(1, peers)
    def _(delta):
        pl.semaphore_signal(
            barrier, inc=1, device_id=(me_d, lax.rem(me_m + delta, peers)), device_id_type=MESH
        )

    def plane_copy(source, landing, phase, delta):
        target = lax.rem(me_d + delta, owners)
        return pltpu.make_async_remote_copy(
            src_ref=source.at[target],
            dst_ref=landing.at[me_d],
            send_sem=send_sem.at[phase],
            recv_sem=recv_sem.at[phase],
            device_id=(target, me_m),
            device_id_type=MESH,
        )

    def plane_send(source, landing, phase):
        @pl.loop(1, owners)
        def _(delta):
            plane_copy(source, landing, phase, delta).start()

        landing[pl.ds(me_d, 1)] = source[pl.ds(me_d, 1)]

    def wait_all(buffer, count, sem):
        held = buffer.at[pl.ds(0, count)]
        pltpu.make_async_copy(held, held, sem).wait()

    u_coded, u_slot, u_first = list_layout(users_ref[...], 128, owners, 0, 0)
    i_coded, i_slot, i_first = list_layout(items_ref[...], 128, owners, 0, SLOTS)
    d_coded, d_slot, d_first = list_layout(days_ref[...], 32, owners, DAY_BASE, DAY_SLOT)
    lists = jnp.zeros((owners, 128), F32)
    for coded, slot in ((u_coded, u_slot), (i_coded, i_slot), (d_coded, d_slot)):
        lists = lists + dot_nt(coded, onehot(slot == iota((128, slot.shape[1]), 0)))
    for owner in range(owners):
        list_out[owner] = lists[owner : owner + 1, :]
    day_t = day_ref[...].T
    table[pl.ds(me_m, 1), :, 0:128] = user_ref[...].astype(BF16)[None]
    table[pl.ds(me_m, 1), :, 128:256] = jnp.zeros((1, 32, 128), BF16)
    table[pl.ds(me_m, 1), :, 128:160] = day_t.astype(BF16)[None]
    table[pl.ds(me_m, 1), :, 256:384] = item_ref[...].astype(BF16)[None]

    pl.semaphore_wait(barrier, owners + peers - 2)

    def table_copy(delta):
        return pltpu.make_async_remote_copy(
            src_ref=table.at[me_m],
            dst_ref=table.at[me_m],
            send_sem=send_sem.at[3],
            recv_sem=recv_sem.at[3],
            device_id=(me_d, lax.rem(me_m + delta, peers)),
            device_id_type=MESH,
        )

    @pl.loop(1, peers)
    def _(delta):
        table_copy(delta).start()

    plane_send(list_out, list_in, 0)

    u_target = u_first + u_slot
    i_target = i_first + i_slot - SLOTS
    d_target = d_first + d_slot

    def column(target):
        n = target.shape[1]
        return jnp.broadcast_to(target.astype(F32), (8, n)).T[:, 0:1].astype(I32)

    u_pick = onehot(column(u_target) == iota((u_target.shape[1], tall), 1))
    i_pick = onehot(column(i_target) == iota((i_target.shape[1], tall), 1))
    d_pick = onehot(column(d_target) == iota((d_target.shape[1], tall), 1))

    wait_all(list_in, owners - 1, recv_sem.at[0])
    wanted = jnp.concatenate([list_in[b] for b in range(owners)], axis=0)
    wanted_t = wanted.T.astype(I32) - 1
    for b in range(owners):
        rows = slice(b * SLOTS, (b + 1) * SLOTS)
        serve_ud[rows, :] = onehot(wanted_t[0:SLOTS, b : b + 1] == iota((SLOTS, 256), 1))
        serve_it[rows, :] = onehot(wanted_t[SLOTS : 2 * SLOTS, b : b + 1] == iota((SLOTS, 128), 1))

    wait_all(table, peers - 1, recv_sem.at[3])
    full = table[...].reshape(-1, ROWS)
    row_out[:, 0:SLOTS, :] = dot_nt(serve_ud[...], full[:, 0:256]).astype(BF16).reshape(owners, SLOTS, -1)
    row_out[:, SLOTS:, :] = dot_nt(serve_it[...], full[:, 256:384]).astype(BF16).reshape(owners, SLOTS, -1)
    plane_send(row_out, row_in, 1)

    serve_ud_t = serve_ud[...].astype(F32).T.astype(BF16)
    serve_it_t = serve_it[...].astype(F32).T.astype(BF16)
    wait_all(row_in, owners - 1, recv_sem.at[1])

    arrived_ud = row_in[:, 0:SLOTS, :].reshape(tall, -1)
    arrived_it = row_in[:, SLOTS:, :].reshape(tall, -1)
    users_f = dot(u_pick, arrived_ud)
    items_f = dot(i_pick, arrived_it)
    user_rows[...] = users_f.astype(BF16)
    user_rows_t[...] = users_f.T.astype(BF16)
    item_rows[...] = items_f.astype(BF16)
    item_half[...] = (0.5 * items_f).astype(BF16)
    day_rows[...] = dot(d_pick, arrived_ud)
    user_acc[...] = jnp.zeros_like(user_acc)
    item_acc[...] = jnp.zeros_like(item_acc)

    @pl.loop(0, CHUNKS)
    def _(chunk):
        status_copy(chunk).wait()
        first = pl.multiple_of(chunk * per_chunk, per_chunk)
        rows = day_rows[pl.ds(first, per_chunk), :]
        users = user_rows[...]
        users_wide = users.astype(F32)
        users_t = user_rows_t[...]
        items = item_rows[...]
        half = item_half[...]
        slopes = []
        spread = []
        sums = []
        for k in range(per_chunk):
            row = rows[k : k + 1, :]
            logits = dot_nt(users * row.astype(BF16), half)
            kind = status_ref[first + k].astype(F32)
            slope = (kind * (jnp.tanh(logits) + (2.0 * kind - 3.0))).astype(BF16)
            projected = dot(slope, items)
            user_acc[...] += projected * row
            sums.append(jnp.sum(projected * users_wide, axis=0, keepdims=True))
            slopes.append(slope)
            spread.append(users_t * jnp.broadcast_to(row, (8, row.shape[1])).T[:, 0:1].astype(BF16))
        day_acc[pl.ds(first, per_chunk), :] = jnp.concatenate(sums, axis=0)
        item_acc[...] += dot(jnp.concatenate(spread, axis=1), jnp.concatenate(slopes, axis=0))

    u_place = onehot(u_target == iota((tall, u_target.shape[1]), 0))
    i_place = onehot(i_target == iota((tall, i_target.shape[1]), 0))
    d_place = onehot(d_target == iota((tall, d_target.shape[1]), 0))
    placed = dot(u_place, user_acc[...].astype(BF16)) + dot(d_place, day_acc[...].astype(BF16))
    slope_out[:, 0:SLOTS, :] = placed.astype(BF16).reshape(owners, SLOTS, -1)
    placed = dot_nt(i_place, item_acc[...].astype(BF16))
    slope_out[:, SLOTS:, :] = placed.astype(BF16).reshape(owners, SLOTS, -1)
    plane_send(slope_out, slope_in, 2)
    wait_all(slope_in, owners - 1, recv_sem.at[2])

    part_ud = dot(serve_ud_t, slope_in[:, 0:SLOTS, :].reshape(tall, -1))
    part_it = dot(serve_it_t, slope_in[:, SLOTS:, :].reshape(tall, -1))
    part_out[:, :, 0:256] = part_ud.T.astype(BF16).reshape(peers, -1, 256)
    part_out[:, :, 256:384] = part_it.T.astype(BF16).reshape(peers, -1, 128)

    def part_copy(delta):
        target = lax.rem(me_m + delta, peers)
        return pltpu.make_async_remote_copy(
            src_ref=part_out.at[target],
            dst_ref=part_in.at[me_m],
            send_sem=send_sem.at[4],
            recv_sem=recv_sem.at[4],
            device_id=(me_d, target),
            device_id_type=MESH,
        )

    @pl.loop(1, peers)
    def _(delta):
        part_copy(delta).start()

    part_in[pl.ds(me_m, 1)] = part_out[pl.ds(me_m, 1)]
    wait_all(part_in, peers - 1, recv_sem.at[4])
    total = part_in[0].astype(F32)
    for m in range(1, peers):
        total = total + part_in[m].astype(F32)
    grad_ref[...] = total * (1.0 / 32.0)

    wait_all(list_out, owners - 1, send_sem.at[0])
    wait_all(row_out, owners - 1, send_sem.at[1])
    wait_all(slope_out, owners - 1, send_sem.at[2])
    wait_all(table, peers - 1, send_sem.at[3])
    wait_all(part_out, peers - 1, send_sem.at[4])


def adam_kernel(grad_ref, *refs):
    arguments, results = refs[:9], refs[9:]
    grads = (
        grad_ref[:, 0:128],
        grad_ref[:, 256:384],
        grad_ref[:, 128:256].T[0:32, :],
    )
    for which, grad in enumerate(grads):
        factor, first, second = (ref[...] for ref in arguments[3 * which : 3 * which + 3])
        first_new = beta_one * first + (1.0 - beta_one) * grad
        second_new = beta_two * second + (1.0 - beta_two) * grad * grad
        change = learn_rate * (first_new / bias_one) / (jnp.sqrt(second_new / bias_two) + epsilon)
        results[3 * which][...] = factor - change
        results[3 * which + 1][...] = first_new
        results[3 * which + 2][...] = second_new


def local(
    users_list,
    items_list,
    days_list,
    status,
    user_factor,
    user_first,
    user_second,
    item_factor,
    item_first,
    item_second,
    day_factor,
    day_first,
    day_second,
):
    owners = lax.axis_size("dp")
    peers = lax.axis_size("mp")
    rank = user_factor.shape[1] * peers
    users, items, days = users_list.shape[1], items_list.shape[1], days_list.shape[1]
    own = user_factor.shape[1]
    tall = owners * SLOTS
    vmem = pl.BlockSpec(memory_space=pltpu.VMEM)
    grad = pl.pallas_call(
        functools.partial(step_kernel, owners, peers),
        out_shape=jax.ShapeDtypeStruct((own, ROWS), F32),
        in_specs=[vmem] * 3 + [pl.BlockSpec(memory_space=pl.ANY)] + [vmem] * 3,
        out_specs=vmem,
        scratch_shapes=[
            pltpu.VMEM(status.shape[1:], I32),
            pltpu.VMEM((owners, 1, 128), F32),
            pltpu.VMEM((owners, 1, 128), F32),
            pltpu.VMEM((peers, own, ROWS), BF16),
            pltpu.VMEM((owners, 2 * SLOTS, rank), BF16),
            pltpu.VMEM((owners, 2 * SLOTS, rank), BF16),
            pltpu.VMEM((owners, 2 * SLOTS, rank), BF16),
            pltpu.VMEM((owners, 2 * SLOTS, rank), BF16),
            pltpu.VMEM((peers, own, ROWS), BF16),
            pltpu.VMEM((peers, own, ROWS), BF16),
            pltpu.VMEM((tall, 256), BF16),
            pltpu.VMEM((tall, 128), BF16),
            pltpu.VMEM((users, rank), BF16),
            pltpu.VMEM((rank, users), BF16),
            pltpu.VMEM((items, rank), BF16),
            pltpu.VMEM((items, rank), BF16),
            pltpu.VMEM((days, rank), F32),
            pltpu.VMEM((users, rank), F32),
            pltpu.VMEM((rank, items), F32),
            pltpu.VMEM((days, rank), F32),
            pltpu.SemaphoreType.DMA((CHUNKS,)),
            pltpu.SemaphoreType.DMA((5,)),
            pltpu.SemaphoreType.DMA((5,)),
        ],
        compiler_params=pltpu.CompilerParams(
            collective_id=0, has_side_effects=True, vmem_limit_bytes=50 << 20
        ),
        name="step",
    )(users_list, items_list, days_list, status, user_factor.T, item_factor.T, day_factor)
    tables = [
        user_factor.T,
        user_first.T,
        user_second.T,
        item_factor.T,
        item_first.T,
        item_second.T,
        day_factor,
        day_first,
        day_second,
    ]
    new = pl.pallas_call(
        adam_kernel,
        out_shape=[jax.ShapeDtypeStruct(table.shape, F32) for table in tables],
        in_specs=[vmem] * 10,
        out_specs=[vmem] * 9,
        name="adam",
    )(grad, *tables)
    return tuple(x.T for x in new[:6]) + tuple(new[6:])


def solution(mesh):
    lists = P(("dp", "mp"), None)
    rows = P("dp", "mp")
    return jax.shard_map(
        local,
        mesh=mesh,
        in_specs=(lists,) * 3 + (P(("dp", "mp"), None, None, None),) + (rows,) * 9,
        out_specs=(rows,) * 9,
        check_vma=False,
    )
```

time: 254 us -> 54.5 us (0.21)
  local copies, waits for them, and re-layouts: 85.5 us -> 4.76 us
  blocking collectives: 54.6 us -> 0 us
  Pallas kernels: 0 us -> 48.7 us
  waiting for transfers between devices: 34.1 us -> 0 us
  starting transfers between devices: 32.5 us -> 0 us
  other arithmetic: 31 us -> 0 us
  matrix products: 13.9 us -> 0 us
    pallas_call x0 -> x2, Pallas kernels: none -> 48.7 us  [the longest x1 47.1 us: local(): pl.pallas_call(functools.partial(step_kernel, owners, peers), out_shape=j...]
    all_gather x3 -> x0, blocking collectives: 38.1 us -> none  [the longest x1 16.3 us: local(): lax.all_gather(days_list, 'mp', axis=0, tiled=True)]
    all_to_all x4 -> x0, waiting for transfers between devices: 34.1 us -> none  [the longest x1 15.4 us: local(): lax.all_to_all(lax.all_to_all(slot_storage.astype(jnp.bfloat16), 'dp', sp...]
    all_to_all x4 -> x0, starting transfers between devices: 32.5 us -> none  [the longest x1 18.8 us: collect_needed_lines(): lax.all_to_all(build_needed_catalogs(desired_line_catalogs, locally_kept_...]
    unnamed x74 -> x14, local copies, waits for them, and re-layouts: 29.4 us -> 4.76 us
    gather x5 -> x0, local copies, waits for them, and re-layouts: 20.1 us -> none  [serve_needed_lines(): jnp.take(loading_table, jnp.clip(wanted, 0, loading_table.shape[0] - 1),...]
    all_to_all x1 -> x0, blocking collectives: 16.5 us -> none  [local(): lax.all_to_all(slot_storage.astype(jnp.bfloat16), 'dp', split_axis=0, con...]
    scatter x1 -> x0, local copies, waits for them, and re-layouts: 15.1 us -> none  [build_needed_catalogs(): blank_slots.at[holder_index, blocks, slot_position_index].set(local_row)]
  transfers between devices with their start and end apart: 4 -> 0, of which waited for: 4 -> 0; matrix products, arithmetic and copies ran while one was open for 5% -> 0% of each run, Pallas kernels for 0% -> 0%
where the time goes in v1:
time: 54.5 us; the launch traced here: 54.1 us
  Pallas kernels  48.7 us (89%)
  local copies, waits for them, and re-layouts  4.76 us (9%)
  between operations  0.67 us (1%)
    pallas_call x1, Pallas kernels, local(): pl.pallas_call(functools.partial(step_kernel, owners, peers), out_shape=j...  47.1 us
    unnamed x14, local copies, waits for them, and re-layouts  4.76 us
    pallas_call x1, Pallas kernels, local(): pl.pallas_call(adam_kernel, out_shape=[jax.ShapeDtypeStruct(table.shape,...  1.6 us

profile of v1, /device:TPU:1, one launch (start us, length us, event | category | flops | bytes accessed | tf_op | source)
XLA Modules:
  0.0 54.1 jit_solution(1525854159030428732)
XLA Ops:
  0.6 0.0 copy-start.1
  0.7 0.7 %copy-done.1 = f32[128,32]{0,1:T(8,128)S(1)} copy-done((f32[128,32]{0,1:T(8,128)S(1)}, f32[128,32]{0,1:T(8,128)}, u32[]{:S(2)}) %copy-start.1) | copy-done | bytes 16408
  1.4 0.0 copy-start.2
  1.4 0.7 %copy-done.2 = f32[128,32]{0,1:T(8,128)S(1)} copy-done((f32[128,32]{0,1:T(8,128)S(1)}, f32[128,32]{0,1:T(8,128)}, u32[]{:S(2)}) %copy-start.2) | copy-done | bytes 16408
  2.1 0.0 copy-start.3
  2.1 0.7 %copy-done.3 = f32[32,32]{1,0:T(8,128)S(1)} copy-done((f32[32,32]{1,0:T(8,128)S(1)}, f32[32,32]{1,0:T(8,128)}, u32[]{:S(2)}) %copy-start.3) | copy-done | bytes 4120
  2.8 0.0 copy-start.4
  2.8 0.7 %copy-done.4 = s32[1,256]{1,0:T(1,128)S(1)} copy-done((s32[1,256]{1,0:T(1,128)S(1)}, s32[1,256]{1,0:T(1,128)}, u32[]{:S(2)}) %copy-start.4) | copy-done | bytes 1048
  3.5 0.0 copy-start.5
  3.5 0.7 %copy-done.5 = s32[1,256]{1,0:T(1,128)S(1)} copy-done((s32[1,256]{1,0:T(1,128)S(1)}, s32[1,256]{1,0:T(1,128)}, u32[]{:S(2)}) %copy-start.5) | copy-done | bytes 1048
  4.2 0.0 copy-start.6
  4.2 0.7 %copy-done.6 = s32[1,32]{1,0:T(1,128)S(1)} copy-done((s32[1,32]{1,0:T(1,128)S(1)}, s32[1,32]{1,0:T(1,128)}, u32[]{:S(2)}) %copy-start.6) | copy-done | bytes 152
  4.8 47.1 %step.1.grad_ref = f32[32,384]{1,0:T(8,128)S(1)} custom-call(s32[1,256]{1,0:T(1,128)S(1)} %copy-done.4, s32[1,256]{1,0:T(1,128)S(1)} %copy-done.5, s32[1,32]{1,0:T(1,128)S(1)} %copy-done.6, s32[1,32,256,256]{3,2,1,0:T(8,128)} %status_hbm.1, f32[32,128]{1,0:T(8,128)S(1)} %bitcast.13, f32[32,128]{1,0:T(8,128)S(1)} %bitcast.15, f32[32,32]{1,0:T(8,128)S(1)} %copy-done.3), custom_call_target="tpu_custom_call" | custom-call | tf_op jit(solution)/shard_map/step/pallas_call | solution.py:324
  51.9 0.0 copy-start
  51.9 0.6 %copy-done = f32[32,384]{1,0:T(8,128)} copy-done((f32[32,384]{1,0:T(8,128)}, f32[32,384]{1,0:T(8,128)S(1)}, u32[]{:S(2)}) %copy-start) | copy-done | bytes 49176
  52.5 1.6 %adam.1 = (f32[32,128]{1,0:T(8,128)}, f32[32,128]{1,0:T(8,128)}, f32[32,128]{1,0:T(8,128)}, f32[32,128]{1,0:T(8,128)}, f32[32,128]{1,0:T(8,128)}, /*index=5*/f32...) custom-call(f32[32,384]{1,0:T(8,128)} %copy-done, f32[32,128]{1,0:T(8,128)} %bitcast.12, ...), custom_call_target="tpu_custom_call" | custom-call | tf_op jit(solution)/shard_map/adam/pallas_call | solution.py:370
Async XLA Ops:
  0.6 0.7 %copy-start.1 = (f32[128,32]{0,1:T(8,128)S(1)}, f32[128,32]{0,1:T(8,128)}, u32[]{:S(2)}) copy-start(f32[128,32]{0,1:T(8,128)} %param.17) | copy-start | bytes 49156
  1.4 0.7 %copy-start.2 = (f32[128,32]{0,1:T(8,128)S(1)}, f32[128,32]{0,1:T(8,128)}, u32[]{:S(2)}) copy-start(f32[128,32]{0,1:T(8,128)} %param.20) | copy-start | bytes 49156
  2.1 0.7 %copy-start.3 = (f32[32,32]{1,0:T(8,128)S(1)}, f32[32,32]{1,0:T(8,128)}, u32[]{:S(2)}) copy-start(f32[32,32]{1,0:T(8,128)} %refs_6_.1) | copy-start | bytes 12292
  2.8 0.7 %copy-start.4 = (s32[1,256]{1,0:T(1,128)S(1)}, s32[1,256]{1,0:T(1,128)}, u32[]{:S(2)}) copy-start(s32[1,256]{1,0:T(1,128)} %users_ref.1) | copy-start | bytes 3076
  3.5 0.7 %copy-start.5 = (s32[1,256]{1,0:T(1,128)S(1)}, s32[1,256]{1,0:T(1,128)}, u32[]{:S(2)}) copy-start(s32[1,256]{1,0:T(1,128)} %items_ref.1) | copy-start | bytes 3076
  4.2 0.7 %copy-start.6 = (s32[1,32]{1,0:T(1,128)S(1)}, s32[1,32]{1,0:T(1,128)}, u32[]{:S(2)}) copy-start(s32[1,32]{1,0:T(1,128)} %days_ref.1) | copy-start | bytes 388
  51.9 0.6 %copy-start = (f32[32,384]{1,0:T(8,128)}, f32[32,384]{1,0:T(8,128)S(1)}, u32[]{:S(2)}) copy-start(f32[32,384]{1,0:T(8,128)S(1)} %step.1.grad_ref) | copy-start | bytes 147460

commit v2 on v1

v2 whole, which is shorter than its diff:
```python
import functools

import jax
import jax.numpy as jnp
from jax import lax
from jax.experimental import pallas as pl
from jax.experimental.pallas import tpu as pltpu
from jax.sharding import PartitionSpec as P

MESH = pl.DeviceIdType.MESH
F32, BF16, I32 = jnp.float32, jnp.bfloat16, jnp.int32

beta_one = 0.9
beta_two = 0.99
bias_one = 1.0 - 0.9**10
bias_two = 1.0 - 0.99**10
learn_rate = 0.01
epsilon = 1e-08

SLOTS = 16
DAY_SLOT = 12
DAY_BASE = 128
ROWS = 384
CHUNKS = 4

FAR_FIRST = sorted(
    ((y, x, c) for y in range(4) for x in range(4) for c in range(2) if y or x or c),
    key=lambda step: -(min(step[0], 4 - step[0]) + min(step[1], 4 - step[1])),
)
Z_FAR_FIRST = (4, 3, 5, 2, 6, 1, 7)


def iota(shape, dim):
    return lax.broadcasted_iota(I32, shape, dim)


def onehot(hit):
    return jnp.where(hit, 1.0, 0.0).astype(BF16)


def dot(a, b):
    return jnp.dot(a, b, preferred_element_type=F32)


def dot_nt(a, b):
    return lax.dot_general(a, b, (((1,), (1,)), ((), ())), preferred_element_type=F32)


def list_layout(rows_wanted, per_owner, owners, base, first_slot):
    n = rows_wanted.shape[1]
    owner = rows_wanted // per_owner
    code = (rows_wanted - owner * per_owner + base + 1).astype(F32)
    hit = owner == iota((owners, n), 0)
    before = onehot(iota((n, n), 0) < iota((n, n), 1))
    rank = dot(onehot(hit), before)
    slot = jnp.sum(jnp.where(hit, rank, 0.0), axis=0, keepdims=True).astype(I32) + first_slot
    coded = jnp.where(hit, code, 0.0).astype(BF16)
    return coded, slot, owner * SLOTS


def step_kernel(
    owners,
    peers,
    users_hbm,
    items_hbm,
    days_hbm,
    status_hbm,
    user_hbm,
    item_hbm,
    day_hbm,
    grad_ref,
    users_ref,
    items_ref,
    days_ref,
    user_ref,
    item_ref,
    day_ref,
    status_ref,
    list_out,
    list_in,
    table_ud,
    table_it,
    day_pack,
    day_full,
    rows_ud_out,
    rows_ud_in,
    rows_it_out,
    rows_it_in,
    slopes_ud_out,
    slopes_ud_in,
    slopes_it_out,
    slopes_it_in,
    part_ud_out,
    part_ud_in,
    part_it_out,
    part_it_in,
    serve_ud,
    serve_it,
    serve_ud_t,
    serve_it_t,
    user_rows,
    user_rows_t,
    item_rows,
    item_half,
    day_rows,
    slope_ref,
    user_acc,
    item_acc,
    day_acc,
    status_sem,
    load_sem,
    send_sem,
    recv_sem,
):
    me_d = lax.axis_index("dp")
    me_m = lax.axis_index("mp")
    tall = owners * SLOTS
    days_here = status_ref.shape[0]
    per_chunk = days_here // CHUNKS

    loads = [
        pltpu.make_async_copy(source, landing, load_sem.at[n])
        for n, (source, landing) in enumerate(
            (
                (users_hbm, users_ref),
                (items_hbm, items_ref),
                (days_hbm, days_ref),
                (user_hbm, user_ref),
                (day_hbm, day_ref),
                (item_hbm, item_ref),
            )
        )
    ]
    for load in loads:
        load.start()

    barrier = pltpu.get_barrier_semaphore()

    @pl.loop(1, owners)
    def _(delta):
        pl.semaphore_signal(
            barrier, inc=1, device_id=(lax.rem(me_d + delta, owners), me_m), device_id_type=MESH
        )

    @pl.loop(1, peers)
    def _(delta):
        pl.semaphore_signal(
            barrier, inc=1, device_id=(me_d, lax.rem(me_m + delta, peers)), device_id_type=MESH
        )

    def status_copy(chunk):
        part = pl.ds(chunk * per_chunk, per_chunk)
        return pltpu.make_async_copy(
            status_hbm.at[0, part], status_ref.at[part], status_sem.at[chunk]
        )

    for chunk in range(CHUNKS):
        status_copy(chunk).start()

    here_y, here_x, here_c = me_d // 8, lax.rem(me_d // 2, 4), lax.rem(me_d, 2)

    def plane_send(source, landing, phase):
        for dy, dx, dc in FAR_FIRST:
            y, x, c = lax.rem(here_y + dy, 4), lax.rem(here_x + dx, 4), lax.rem(here_c + dc, 2)
            target = y * 8 + x * 2 + c
            pltpu.make_async_remote_copy(
                src_ref=source.at[target],
                dst_ref=landing.at[me_d],
                send_sem=send_sem.at[phase],
                recv_sem=recv_sem.at[phase],
                device_id=(target, me_m),
                device_id_type=MESH,
            ).start()
        landing[pl.ds(me_d, 1)] = source[pl.ds(me_d, 1)]

    def column_gather(pieces, phase):
        for delta in Z_FAR_FIRST:
            pltpu.make_async_remote_copy(
                src_ref=pieces.at[me_m],
                dst_ref=pieces.at[me_m],
                send_sem=send_sem.at[phase],
                recv_sem=recv_sem.at[phase],
                device_id=(me_d, lax.rem(me_m + delta, peers)),
                device_id_type=MESH,
            ).start()

    def column_scatter(source, landing, phase):
        for delta in Z_FAR_FIRST:
            target = lax.rem(me_m + delta, peers)
            pltpu.make_async_remote_copy(
                src_ref=source.at[target],
                dst_ref=landing.at[me_m],
                send_sem=send_sem.at[phase],
                recv_sem=recv_sem.at[phase],
                device_id=(me_d, target),
                device_id_type=MESH,
            ).start()
        landing[pl.ds(me_m, 1)] = source[pl.ds(me_m, 1)]

    def wait_all(buffer, sem):
        held = buffer.at[pl.ds(0, buffer.shape[0] - 1)]
        pltpu.make_async_copy(held, held, sem).wait()

    for load in loads:
        load.wait()

    table_ud[pl.ds(me_m, 1), 0:32, :] = user_ref[...].astype(BF16)[None]
    table_it[pl.ds(me_m, 1), :, :] = item_ref[...].astype(BF16)[None]
    day_t = day_ref[...].T
    day_pack[...] = jnp.zeros_like(day_pack)
    day_pack[:, 0:32] = day_t[0:16, :]
    day_pack[:, 32:64] = day_t[16:32, :]
    table_ud[pl.ds(me_m, 1), 32:48, :] = day_pack[...].astype(BF16)[None]

    u_coded, u_slot, u_first = list_layout(users_ref[...], 128, owners, 0, 0)
    i_coded, i_slot, i_first = list_layout(items_ref[...], 128, owners, 0, SLOTS)
    d_coded, d_slot, d_first = list_layout(days_ref[...], 32, owners, DAY_BASE, DAY_SLOT)
    lists = jnp.zeros((owners, 128), F32)
    for coded, slot in ((u_coded, u_slot), (i_coded, i_slot), (d_coded, d_slot)):
        lists = lists + dot_nt(coded, onehot(slot == iota((128, slot.shape[1]), 0)))
    for owner in range(owners):
        list_out[owner] = lists[owner : owner + 1, :]

    pl.semaphore_wait(barrier, owners + peers - 2)

    column_gather(table_ud, 0)
    plane_send(list_out, list_in, 2)
    column_gather(table_it, 1)

    u_target = u_first + u_slot
    i_target = i_first + i_slot - SLOTS
    d_target = d_first + d_slot

    def column(target):
        n = target.shape[1]
        return jnp.broadcast_to(target.astype(F32), (8, n)).T[:, 0:1].astype(I32)

    u_pick = onehot(column(u_target) == iota((u_target.shape[1], tall), 1))
    i_pick = onehot(column(i_target) == iota((i_target.shape[1], tall), 1))
    d_pick = onehot(column(d_target) == iota((d_target.shape[1], tall), 1))

    wait_all(list_in, recv_sem.at[2])
    wanted = jnp.concatenate([list_in[b] for b in range(owners)], axis=0)
    wanted_t = wanted.T.astype(I32) - 1
    for b in range(owners):
        rows = slice(b * SLOTS, (b + 1) * SLOTS)
        serve_ud[rows, :] = onehot(wanted_t[0:SLOTS, b : b + 1] == iota((SLOTS, 256), 1))
        serve_it[rows, :] = onehot(wanted_t[SLOTS : 2 * SLOTS, b : b + 1] == iota((SLOTS, 128), 1))

    wait_all(table_ud, recv_sem.at[0])
    for m in range(peers):
        packed = table_ud[m, 32:48, :].astype(F32)
        lane = iota(packed.shape, 1)
        day_full[m, 0:16, :] = jnp.where(lane < 32, packed, 0.0).astype(BF16)
        day_full[m, 16:32, :] = jnp.where(lane < 32, pltpu.roll(packed, 96, 1), 0.0).astype(BF16)
    served = dot_nt(serve_ud[:, 0:128], table_ud[:, 0:32, :].reshape(-1, 128))
    served = served + dot_nt(serve_ud[:, 128:256], day_full[...].reshape(-1, 128))
    rows_ud_out[...] = served.astype(BF16).reshape(owners, SLOTS, -1)
    plane_send(rows_ud_out, rows_ud_in, 3)
    wait_all(table_it, recv_sem.at[1])
    served = dot_nt(serve_it[...], table_it[...].reshape(-1, 128))
    rows_it_out[...] = served.astype(BF16).reshape(owners, SLOTS, -1)
    plane_send(rows_it_out, rows_it_in, 4)

    serve_ud_t[...] = serve_ud[...].astype(F32).T.astype(BF16)
    serve_it_t[...] = serve_it[...].astype(F32).T.astype(BF16)
    user_acc[...] = jnp.zeros_like(user_acc)
    item_acc[...] = jnp.zeros_like(item_acc)
    for chunk in range(CHUNKS):
        status_copy(chunk).wait()

    wait_all(rows_ud_in, recv_sem.at[3])
    arrived = rows_ud_in[...].reshape(tall, -1)
    users_f = dot(u_pick, arrived)
    user_rows[...] = users_f.astype(BF16)
    user_rows_t[...] = users_f.T.astype(BF16)
    day_rows[...] = dot(d_pick, arrived)
    wait_all(rows_it_in, recv_sem.at[4])
    items_f = dot(i_pick, rows_it_in[...].reshape(tall, -1))
    item_rows[...] = items_f.astype(BF16)
    item_half[...] = (0.5 * items_f).astype(BF16)

    @pl.loop(0, CHUNKS)
    def _(chunk):
        first = pl.multiple_of(chunk * per_chunk, per_chunk)
        rows = day_rows[pl.ds(first, per_chunk), :]
        users = user_rows[...]
        users_t = user_rows_t[...]
        half = item_half[...]
        slopes = []
        spread = []
        for k in range(per_chunk):
            row = rows[k : k + 1, :]
            logits = dot_nt(users * row.astype(BF16), half)
            kind = status_ref[first + k].astype(F32)
            slope = (kind * (jnp.tanh(logits) + (2.0 * kind - 3.0))).astype(BF16)
            slope_ref[first + k] = slope
            slopes.append(slope)
            spread.append(users_t * jnp.broadcast_to(row, (8, row.shape[1])).T[:, 0:1].astype(BF16))
        item_acc[...] += dot(jnp.concatenate(spread, axis=1), jnp.concatenate(slopes, axis=0))

    i_place = onehot(i_target == iota((tall, i_target.shape[1]), 0))
    placed = dot_nt(i_place, item_acc[...].astype(BF16))
    slopes_it_out[...] = placed.astype(BF16).reshape(owners, SLOTS, -1)
    plane_send(slopes_it_out, slopes_it_in, 5)

    @pl.loop(0, CHUNKS)
    def _(chunk):
        first = pl.multiple_of(chunk * per_chunk, per_chunk)
        rows = day_rows[pl.ds(first, per_chunk), :]
        users_wide = user_rows[...].astype(F32)
        items = item_rows[...]
        sums = []
        for k in range(per_chunk):
            projected = dot(slope_ref[first + k], items)
            user_acc[...] += projected * rows[k : k + 1, :]
            sums.append(jnp.sum(projected * users_wide, axis=0, keepdims=True))
        day_acc[pl.ds(first, per_chunk), :] = jnp.concatenate(sums, axis=0)

    u_place = onehot(u_target == iota((tall, u_target.shape[1]), 0))
    d_place = onehot(d_target == iota((tall, d_target.shape[1]), 0))
    placed = dot(u_place, user_acc[...].astype(BF16)) + dot(d_place, day_acc[...].astype(BF16))
    slopes_ud_out[...] = placed.astype(BF16).reshape(owners, SLOTS, -1)
    plane_send(slopes_ud_out, slopes_ud_in, 6)

    wait_all(slopes_it_in, recv_sem.at[5])
    part = dot(serve_it_t[...], slopes_it_in[...].reshape(tall, -1))
    part_it_out[...] = part.T.astype(BF16).reshape(peers, -1, 128)
    column_scatter(part_it_out, part_it_in, 7)

    wait_all(slopes_ud_in, recv_sem.at[6])
    part = dot(serve_ud_t[...], slopes_ud_in[...].reshape(tall, -1))
    part_ud_out[:, 0:32, :] = part[0:128, :].T.astype(BF16).reshape(peers, -1, 128)
    day_part = part[128:256, :].T.reshape(peers, 2, 16, 128)
    for m in range(peers):
        part_ud_out[m, 32:48, :] = (day_part[m, 0] + pltpu.roll(day_part[m, 1], 32, 1)).astype(BF16)
    column_scatter(part_ud_out, part_ud_in, 8)

    wait_all(part_it_in, recv_sem.at[7])
    total = part_it_in[0].astype(F32)
    for m in range(1, peers):
        total = total + part_it_in[m].astype(F32)
    grad_ref[:, 256:384] = total * (1.0 / 32.0)
    wait_all(part_ud_in, recv_sem.at[8])
    total = part_ud_in[0].astype(F32)
    for m in range(1, peers):
        total = total + part_ud_in[m].astype(F32)
    total = total * (1.0 / 32.0)
    grad_ref[:, 0:128] = total[0:32, :]
    grad_ref[0:16, 128:256] = total[32:48, :]
    grad_ref[16:32, 128:256] = pltpu.roll(total[32:48, :], 96, 1)

    for phase, buffer in enumerate(
        (
            table_ud,
            table_it,
            list_out,
            rows_ud_out,
            rows_it_out,
            slopes_it_out,
            slopes_ud_out,
            part_it_out,
            part_ud_out,
        )
    ):
        wait_all(buffer, send_sem.at[phase])


def adam_kernel(grad_ref, *refs):
    tables, results, held, made, load_sem, store_sem = (
        refs[:9],
        refs[9:18],
        refs[18:27],
        refs[27:36],
        refs[36],
        refs[37],
    )
    loads = [pltpu.make_async_copy(tables[n], held[n], load_sem.at[n]) for n in range(9)]
    stores = [pltpu.make_async_copy(made[n], results[n], store_sem.at[n]) for n in range(9)]
    for load in loads:
        load.start()
    grads = (
        grad_ref[:, 0:128],
        grad_ref[:, 256:384],
        grad_ref[:, 128:256].T[0:32, :],
    )
    for which, grad in enumerate(grads):
        picked = slice(3 * which, 3 * which + 3)
        for load in loads[picked]:
            load.wait()
        factor, first, second = (ref[...] for ref in held[picked])
        first_new = beta_one * first + (1.0 - beta_one) * grad
        second_new = beta_two * second + (1.0 - beta_two) * grad * grad
        change = learn_rate * (first_new / bias_one) / (jnp.sqrt(second_new / bias_two) + epsilon)
        for ref, value in zip(made[picked], (factor - change, first_new, second_new)):
            ref[...] = value
        for store in stores[picked]:
            store.start()
    for store in stores:
        store.wait()


def local(
    users_list,
    items_list,
    days_list,
    status,
    user_factor,
    user_first,
    user_second,
    item_factor,
    item_first,
    item_second,
    day_factor,
    day_first,
    day_second,
):
    owners = lax.axis_size("dp")
    peers = lax.axis_size("mp")
    rank = user_factor.shape[1] * peers
    users, items, days = users_list.shape[1], items_list.shape[1], days_list.shape[1]
    own = user_factor.shape[1]
    tall = owners * SLOTS
    vmem = pl.BlockSpec(memory_space=pltpu.VMEM)
    hbm = pl.BlockSpec(memory_space=pltpu.HBM)
    slots = pltpu.VMEM((owners, SLOTS, rank), BF16)
    grad = pl.pallas_call(
        functools.partial(step_kernel, owners, peers),
        out_shape=jax.ShapeDtypeStruct((own, ROWS), F32),
        in_specs=[hbm] * 7,
        out_specs=vmem,
        scratch_shapes=[
            pltpu.VMEM(users_list.shape, I32),
            pltpu.VMEM(items_list.shape, I32),
            pltpu.VMEM(days_list.shape, I32),
            pltpu.VMEM((own, user_factor.shape[0]), F32),
            pltpu.VMEM((own, item_factor.shape[0]), F32),
            pltpu.VMEM(day_factor.shape, F32),
            pltpu.VMEM(status.shape[1:], I32),
            pltpu.VMEM((owners, 1, 128), F32),
            pltpu.VMEM((owners, 1, 128), F32),
            pltpu.VMEM((peers, 48, 128), BF16),
            pltpu.VMEM((peers, 32, 128), BF16),
            pltpu.VMEM((16, 128), F32),
            pltpu.VMEM((peers, 32, 128), BF16),
            *[slots] * 8,
            pltpu.VMEM((peers, 48, 128), BF16),
            pltpu.VMEM((peers, 48, 128), BF16),
            pltpu.VMEM((peers, 32, 128), BF16),
            pltpu.VMEM((peers, 32, 128), BF16),
            pltpu.VMEM((tall, 256), BF16),
            pltpu.VMEM((tall, 128), BF16),
            pltpu.VMEM((256, tall), BF16),
            pltpu.VMEM((128, tall), BF16),
            pltpu.VMEM((users, rank), BF16),
            pltpu.VMEM((rank, users), BF16),
            pltpu.VMEM((items, rank), BF16),
            pltpu.VMEM((items, rank), BF16),
            pltpu.VMEM((days, rank), F32),
            pltpu.VMEM((days, users, items), BF16),
            pltpu.VMEM((users, rank), F32),
            pltpu.VMEM((rank, items), F32),
            pltpu.VMEM((days, rank), F32),
            pltpu.SemaphoreType.DMA((CHUNKS,)),
            pltpu.SemaphoreType.DMA((6,)),
            pltpu.SemaphoreType.DMA((9,)),
            pltpu.SemaphoreType.DMA((9,)),
        ],
        compiler_params=pltpu.CompilerParams(
            collective_id=0, has_side_effects=True, vmem_limit_bytes=60 << 20
        ),
        name="step",
    )(users_list, items_list, days_list, status, user_factor.T, item_factor.T, day_factor)
    tables = [
        user_factor.T,
        user_first.T,
        user_second.T,
        item_factor.T,
        item_first.T,
        item_second.T,
        day_factor,
        day_first,
        day_second,
    ]
    new = pl.pallas_call(
        adam_kernel,
        out_shape=[jax.ShapeDtypeStruct(table.shape, F32) for table in tables],
        in_specs=[vmem] + [hbm] * 9,
        out_specs=[hbm] * 9,
        scratch_shapes=[pltpu.VMEM(table.shape, F32) for table in tables] * 2
        + [pltpu.SemaphoreType.DMA((9,))] * 2,
        compiler_params=pltpu.CompilerParams(vmem_limit_bytes=8 << 20),
        name="adam",
    )(grad, *tables)
    return tuple(x.T for x in new[:6]) + tuple(new[6:])


def solution(mesh):
    lists = P(("dp", "mp"), None)
    rows = P("dp", "mp")
    return jax.shard_map(
        local,
        mesh=mesh,
        in_specs=(lists,) * 3 + (P(("dp", "mp"), None, None, None),) + (rows,) * 9,
        out_specs=(rows,) * 9,
        check_vma=False,
    )
```

time: 54.5 us -> 47.9 us (0.88)
  local copies, waits for them, and re-layouts: 4.76 us -> 0.83 us
  Pallas kernels: 48.7 us -> 46.1 us
    unnamed x14 -> x20, local copies, waits for them, and re-layouts: 4.76 us -> 0.83 us
    pallas_call x1, Pallas kernels: 47.1 us -> 45 us  [local(): pl.pallas_call(functools.partial(step_kernel, owners, peers), out_shape=j...]
where the time goes in v2:
time: 47.9 us; the launch traced here: 47.7 us
  Pallas kernels  46.1 us (96%)
  local copies, waits for them, and re-layouts  0.83 us (2%)
  between operations  0.81 us (2%)
    pallas_call x1, Pallas kernels, local(): pl.pallas_call(functools.partial(step_kernel, owners, peers), out_shape=j...  45 us
    pallas_call x1, Pallas kernels, local(): pl.pallas_call(adam_kernel, out_shape=[jax.ShapeDtypeStruct(table.shape,...  1.1 us

profile of v2, /device:TPU:1, one launch (start us, length us, event | category | flops | bytes accessed | tf_op | source)
XLA Modules:
  0.0 47.7 jit_solution(18199157986326801768)
XLA Ops:
  0.6 0.0 copy-start.3
  0.7 0.0 copy-start.9
  0.7 0.0 copy-start.8
  0.7 0.0 copy-start.7
  0.7 0.0 copy-start.6
  0.7 0.0 copy-start.2
  0.7 0.0 copy-start.5
  0.7 0.0 copy-start.4
  0.7 0.0 copy-start.1
  0.7 45.0 %step.1.grad_ref = f32[32,384]{1,0:T(8,128)} custom-call(s32[1,256]{1,0:T(1,128)} %users_hbm.1, s32[1,256]{1,0:T(1,128)} %items_hbm.1, s32[1,32]{1,0:T(1,128)} %days_hbm.1, s32[1,32,256,256]{3,2,1,0:T(8,128)} %status_hbm.1, f32[32,128]{1,0:T(8,128)} %bitcast.12, f32[32,128]{1,0:T(8,128)} %bitcast.14, f32[32,32]{1,0:T(8,128)} %refs_6_.1), custom_call_target="tpu_custom_call" | custom-call | tf_op jit(solution)/shard_map/step/pallas_call | solution.py:427
  45.7 0.0 copy-done.3
  45.8 0.0 copy-done.9
  45.8 0.0 copy-done.8
  45.8 0.0 copy-done.7
  45.8 0.0 copy-done.6
  45.8 0.0 copy-done.2
  45.8 0.0 copy-done.5
  45.8 0.0 copy-done.4
  45.8 0.0 copy-done.1
  45.8 0.0 copy-start
  45.8 0.8 %copy-done = f32[32,384]{1,0:T(8,128)S(1)} copy-done((f32[32,384]{1,0:T(8,128)S(1)}, f32[32,384]{1,0:T(8,128)}, u32[]{:S(2)}) %copy-start) | copy-done | bytes 49176
  46.6 1.1 %adam.1 = (f32[32,128]{1,0:T(8,128)}, f32[32,128]{1,0:T(8,128)}, f32[32,128]{1,0:T(8,128)}, f32[32,128]{1,0:T(8,128)}, f32[32,128]{1,0:T(8,128)}, /*index=5*/f32...) custom-call(f32[32,384]{1,0:T(8,128)S(1)} %copy-done, f32[32,128]{1,0:T(8,128)S(1)} %bitcast.13, ...), custom_call_target="tpu_custom_call" | custom-call | tf_op jit(solution)/shard_map/adam/pallas_call | solution.py:485
Async XLA Ops:
  0.6 45.1 %copy-start.3 = (f32[32,32]{1,0:T(8,128)S(1)}, f32[32,32]{1,0:T(8,128)}, u32[]{:S(2)}) copy-start(f32[32,32]{1,0:T(8,128)} %refs_6_.1) | copy-start | bytes 12292
  0.7 45.1 %copy-start.9 = (f32[32,32]{1,0:T(8,128)S(1)}, f32[32,32]{1,0:T(8,128)}, u32[]{:S(2)}) copy-start(f32[32,32]{1,0:T(8,128)} %refs_8_.1) | copy-start | bytes 12292
  0.7 45.1 %copy-start.8 = (f32[32,32]{1,0:T(8,128)S(1)}, f32[32,32]{1,0:T(8,128)}, u32[]{:S(2)}) copy-start(f32[32,32]{1,0:T(8,128)} %refs_7_.1) | copy-start | bytes 12292
  0.7 45.1 %copy-start.7 = (f32[128,32]{0,1:T(8,128)S(1)}, f32[128,32]{0,1:T(8,128)}, u32[]{:S(2)}) copy-start(f32[128,32]{0,1:T(8,128)} %param.22) | copy-start | bytes 49156
  0.7 45.1 %copy-start.6 = (f32[128,32]{0,1:T(8,128)S(1)}, f32[128,32]{0,1:T(8,128)}, u32[]{:S(2)}) copy-start(f32[128,32]{0,1:T(8,128)} %param.21) | copy-start | bytes 49156
  0.7 45.1 %copy-start.2 = (f32[128,32]{0,1:T(8,128)S(1)}, f32[128,32]{0,1:T(8,128)}, u32[]{:S(2)}) copy-start(f32[128,32]{0,1:T(8,128)} %param.20) | copy-start | bytes 49156
  0.7 45.1 %copy-start.5 = (f32[128,32]{0,1:T(8,128)S(1)}, f32[128,32]{0,1:T(8,128)}, u32[]{:S(2)}) copy-start(f32[128,32]{0,1:T(8,128)} %param.19) | copy-start | bytes 49156
  0.7 45.1 %copy-start.4 = (f32[128,32]{0,1:T(8,128)S(1)}, f32[128,32]{0,1:T(8,128)}, u32[]{:S(2)}) copy-start(f32[128,32]{0,1:T(8,128)} %param.18) | copy-start | bytes 49156
  0.7 45.1 %copy-start.1 = (f32[128,32]{0,1:T(8,128)S(1)}, f32[128,32]{0,1:T(8,128)}, u32[]{:S(2)}) copy-start(f32[128,32]{0,1:T(8,128)} %param.17) | copy-start | bytes 49156
  45.8 0.8 %copy-start = (f32[32,384]{1,0:T(8,128)S(1)}, f32[32,384]{1,0:T(8,128)}, u32[]{:S(2)}) copy-start(f32[32,384]{1,0:T(8,128)} %step.1.grad_ref) | copy-start | bytes 147460

commit v3 on v2

--- a/solution.py
+++ b/solution.py
@@ -99,7 +99,7 @@
     serve_ud_t,
     serve_it_t,
     user_rows,
-    user_rows_t,
+    spread,
     item_rows,
     item_half,
     day_rows,
@@ -114,10 +114,6 @@
 ):
     me_d = lax.axis_index("dp")
     me_m = lax.axis_index("mp")
-    tall = owners * SLOTS
-    days_here = status_ref.shape[0]
-    per_chunk = days_here // CHUNKS
-
     loads = [
         pltpu.make_async_copy(source, landing, load_sem.at[n])
         for n, (source, landing) in enumerate(
@@ -133,6 +129,9 @@
     ]
     for load in loads:
         load.start()
+    tall = owners * SLOTS
+    days_here, users_count, items_count = status_ref.shape
+    per_chunk = days_here // CHUNKS
 
     barrier = pltpu.get_barrier_semaphore()
 
@@ -205,12 +204,14 @@
         load.wait()
 
     table_ud[pl.ds(me_m, 1), 0:32, :] = user_ref[...].astype(BF16)[None]
+    day_t = day_ref[...].T
+    for q in range(4):
+        day_pack[:, 32 * q : 32 * q + 32] = day_t[8 * q : 8 * q + 8, :]
+    table_ud[pl.ds(me_m, 1), 32:40, :] = day_pack[...].astype(BF16)[None]
     table_it[pl.ds(me_m, 1), :, :] = item_ref[...].astype(BF16)[None]
-    day_t = day_ref[...].T
-    day_pack[...] = jnp.zeros_like(day_pack)
-    day_pack[:, 0:32] = day_t[0:16, :]
-    day_pack[:, 32:64] = day_t[16:32, :]
-    table_ud[pl.ds(me_m, 1), 32:48, :] = day_pack[...].astype(BF16)[None]
+
+    pl.semaphore_wait(barrier, owners + peers - 2)
+    column_gather(table_ud, 0)
 
     u_coded, u_slot, u_first = list_layout(users_ref[...], 128, owners, 0, 0)
     i_coded, i_slot, i_first = list_layout(items_ref[...], 128, owners, 0, SLOTS)
@@ -221,9 +222,6 @@
     for owner in range(owners):
         list_out[owner] = lists[owner : owner + 1, :]
 
-    pl.semaphore_wait(barrier, owners + peers - 2)
-
-    column_gather(table_ud, 0)
     plane_send(list_out, list_in, 2)
     column_gather(table_it, 1)
 
@@ -248,13 +246,13 @@
         serve_it[rows, :] = onehot(wanted_t[SLOTS : 2 * SLOTS, b : b + 1] == iota((SLOTS, 128), 1))
 
     wait_all(table_ud, recv_sem.at[0])
-    for m in range(peers):
-        packed = table_ud[m, 32:48, :].astype(F32)
-        lane = iota(packed.shape, 1)
-        day_full[m, 0:16, :] = jnp.where(lane < 32, packed, 0.0).astype(BF16)
-        day_full[m, 16:32, :] = jnp.where(lane < 32, pltpu.roll(packed, 96, 1), 0.0).astype(BF16)
+    packed = table_ud[:, 32:40, :].astype(F32).reshape(-1, 128)
+    lane = iota(packed.shape, 1)
+    for q in range(4):
+        turned = packed if q == 0 else pltpu.roll(packed, 128 - 32 * q, 1)
+        day_full[:, 8 * q : 8 * q + 8, :] = jnp.where(lane < 32, turned, 0.0).reshape(-1, 8, 128)
     served = dot_nt(serve_ud[:, 0:128], table_ud[:, 0:32, :].reshape(-1, 128))
-    served = served + dot_nt(serve_ud[:, 128:256], day_full[...].reshape(-1, 128))
+    served = served + dot_nt(serve_ud[:, 128:256], day_full[...].astype(BF16).reshape(-1, 128))
     rows_ud_out[...] = served.astype(BF16).reshape(owners, SLOTS, -1)
     plane_send(rows_ud_out, rows_ud_in, 3)
     wait_all(table_it, recv_sem.at[1])
@@ -273,49 +271,55 @@
     arrived = rows_ud_in[...].reshape(tall, -1)
     users_f = dot(u_pick, arrived)
     user_rows[...] = users_f.astype(BF16)
-    user_rows_t[...] = users_f.T.astype(BF16)
     day_rows[...] = dot(d_pick, arrived)
+    rows_t = day_rows[...].T
+    users_t = users_f.T.astype(BF16)
+    for k in range(days_here):
+        spread[:, k * users_count : (k + 1) * users_count] = users_t * rows_t[:, k : k + 1].astype(BF16)
     wait_all(rows_it_in, recv_sem.at[4])
     items_f = dot(i_pick, rows_it_in[...].reshape(tall, -1))
     item_rows[...] = items_f.astype(BF16)
     item_half[...] = (0.5 * items_f).astype(BF16)
 
-    @pl.loop(0, CHUNKS)
-    def _(chunk):
-        first = pl.multiple_of(chunk * per_chunk, per_chunk)
-        rows = day_rows[pl.ds(first, per_chunk), :]
+    def make_slopes(chunk):
         users = user_rows[...]
-        users_t = user_rows_t[...]
         half = item_half[...]
-        slopes = []
-        spread = []
-        for k in range(per_chunk):
-            row = rows[k : k + 1, :]
-            logits = dot_nt(users * row.astype(BF16), half)
-            kind = status_ref[first + k].astype(F32)
-            slope = (kind * (jnp.tanh(logits) + (2.0 * kind - 3.0))).astype(BF16)
-            slope_ref[first + k] = slope
-            slopes.append(slope)
-            spread.append(users_t * jnp.broadcast_to(row, (8, row.shape[1])).T[:, 0:1].astype(BF16))
-        item_acc[...] += dot(jnp.concatenate(spread, axis=1), jnp.concatenate(slopes, axis=0))
+        for k in range(chunk * per_chunk, (chunk + 1) * per_chunk):
+            logits = dot_nt(users * day_rows[k : k + 1, :].astype(BF16), half)
+            kind = status_ref[k].astype(F32)
+            slope_ref[k] = (kind * (jnp.tanh(logits) + (2.0 * kind - 3.0))).astype(BF16)
+
+    def chunk_slopes(chunk):
+        return slope_ref[chunk * per_chunk : (chunk + 1) * per_chunk].reshape(-1, items_count)
+
+    def add_items(chunk):
+        width = per_chunk * users_count
+        item_acc[...] += dot(spread[:, chunk * width : (chunk + 1) * width], chunk_slopes(chunk))
+
+    make_slopes(0)
+    for chunk in range(1, CHUNKS):
+        add_items(chunk - 1)
+        make_slopes(chunk)
+    add_items(CHUNKS - 1)
 
     i_place = onehot(i_target == iota((tall, i_target.shape[1]), 0))
     placed = dot_nt(i_place, item_acc[...].astype(BF16))
     slopes_it_out[...] = placed.astype(BF16).reshape(owners, SLOTS, -1)
     plane_send(slopes_it_out, slopes_it_in, 5)
 
-    @pl.loop(0, CHUNKS)
-    def _(chunk):
-        first = pl.multiple_of(chunk * per_chunk, per_chunk)
-        rows = day_rows[pl.ds(first, per_chunk), :]
-        users_wide = user_rows[...].astype(F32)
-        items = item_rows[...]
+    users_wide = user_rows[...].astype(F32)
+    items = item_rows[...]
+    for chunk in range(CHUNKS):
+        projected = dot(chunk_slopes(chunk), items)
+        acc = user_acc[...]
         sums = []
-        for k in range(per_chunk):
-            projected = dot(slope_ref[first + k], items)
-            user_acc[...] += projected * rows[k : k + 1, :]
-            sums.append(jnp.sum(projected * users_wide, axis=0, keepdims=True))
-        day_acc[pl.ds(first, per_chunk), :] = jnp.concatenate(sums, axis=0)
+        for n in range(per_chunk):
+            k = chunk * per_chunk + n
+            part = projected[n * users_count : (n + 1) * users_count]
+            acc = acc + part * day_rows[k : k + 1, :]
+            sums.append(jnp.sum(part * users_wide, axis=0, keepdims=True))
+        user_acc[...] = acc
+        day_acc[chunk * per_chunk : (chunk + 1) * per_chunk, :] = jnp.concatenate(sums, axis=0)
 
     u_place = onehot(u_target == iota((tall, u_target.shape[1]), 0))
     d_place = onehot(d_target == iota((tall, d_target.shape[1]), 0))
@@ -331,9 +335,11 @@
     wait_all(slopes_ud_in, recv_sem.at[6])
     part = dot(serve_ud_t[...], slopes_ud_in[...].reshape(tall, -1))
     part_ud_out[:, 0:32, :] = part[0:128, :].T.astype(BF16).reshape(peers, -1, 128)
-    day_part = part[128:256, :].T.reshape(peers, 2, 16, 128)
-    for m in range(peers):
-        part_ud_out[m, 32:48, :] = (day_part[m, 0] + pltpu.roll(day_part[m, 1], 32, 1)).astype(BF16)
+    day_part = part[128:256, :].T.reshape(peers, 4, 8, 128)
+    packed = day_part[:, 0].reshape(-1, 128)
+    for q in range(1, 4):
+        packed = packed + pltpu.roll(day_part[:, q].reshape(-1, 128), 32 * q, 1)
+    part_ud_out[:, 32:40, :] = packed.astype(BF16).reshape(peers, 8, 128)
     column_scatter(part_ud_out, part_ud_in, 8)
 
     wait_all(part_it_in, recv_sem.at[7])
@@ -347,8 +353,10 @@
         total = total + part_ud_in[m].astype(F32)
     total = total * (1.0 / 32.0)
     grad_ref[:, 0:128] = total[0:32, :]
-    grad_ref[0:16, 128:256] = total[32:48, :]
-    grad_ref[16:32, 128:256] = pltpu.roll(total[32:48, :], 96, 1)
+    packed = total[32:40, :]
+    grad_ref[0:8, 128:256] = packed
+    for q in range(1, 4):
+        grad_ref[8 * q : 8 * q + 8, 128:256] = pltpu.roll(packed, 128 - 32 * q, 1)
 
     for phase, buffer in enumerate(
         (
@@ -439,13 +447,13 @@
             pltpu.VMEM(status.shape[1:], I32),
             pltpu.VMEM((owners, 1, 128), F32),
             pltpu.VMEM((owners, 1, 128), F32),
-            pltpu.VMEM((peers, 48, 128), BF16),
+            pltpu.VMEM((peers, 40, 128), BF16),
             pltpu.VMEM((peers, 32, 128), BF16),
-            pltpu.VMEM((16, 128), F32),
-            pltpu.VMEM((peers, 32, 128), BF16),
+            pltpu.VMEM((8, 128), F32),
+            pltpu.VMEM((peers, 32, 128), F32),
             *[slots] * 8,
-            pltpu.VMEM((peers, 48, 128), BF16),
-            pltpu.VMEM((peers, 48, 128), BF16),
+            pltpu.VMEM((peers, 40, 128), BF16),
+            pltpu.VMEM((peers, 40, 128), BF16),
             pltpu.VMEM((peers, 32, 128), BF16),
             pltpu.VMEM((peers, 32, 128), BF16),
             pltpu.VMEM((tall, 256), BF16),
@@ -453,7 +461,7 @@
             pltpu.VMEM((256, tall), BF16),
             pltpu.VMEM((128, tall), BF16),
             pltpu.VMEM((users, rank), BF16),
-            pltpu.VMEM((rank, users), BF16),
+            pltpu.VMEM((rank, days * users), BF16),
             pltpu.VMEM((items, rank), BF16),
             pltpu.VMEM((items, rank), BF16),
             pltpu.VMEM((days, rank), F32),

time: 47.9 us -> 45 us (0.939)
  Pallas kernels: 46.1 us -> 43.1 us
    pallas_call x1, Pallas kernels: 45 us -> 42 us  [local(): pl.pallas_call(functools.partial(step_kernel, owners, peers), out_shape=j...]
where the time goes in v3:
time: 45 us; the launch traced here: 44.8 us
  Pallas kernels  43.1 us (96%)
  local copies, waits for them, and re-layouts  0.83 us (2%)
  between operations  0.81 us (2%)
    pallas_call x1, Pallas kernels, local(): pl.pallas_call(functools.partial(step_kernel, owners, peers), out_shape=j...  42 us
    pallas_call x1, Pallas kernels, local(): pl.pallas_call(adam_kernel, out_shape=[jax.ShapeDtypeStruct(table.shape,...  1.1 us

profile of v3, /device:TPU:1, one launch (start us, length us, event | category | flops | bytes accessed | tf_op | source)
XLA Modules:
  0.0 44.8 jit_solution(18021227738192998360)
XLA Ops:
  0.6 0.0 copy-start.3
  0.7 0.0 copy-start.9
  0.7 0.0 copy-start.8
  0.7 0.0 copy-start.7
  0.7 0.0 copy-start.6
  0.7 0.0 copy-start.2
  0.7 0.0 copy-start.5
  0.7 0.0 copy-start.4
  0.7 0.0 copy-start.1
  0.7 42.0 %step.1.grad_ref = f32[32,384]{1,0:T(8,128)} custom-call(s32[1,256]{1,0:T(1,128)} %users_hbm.1, s32[1,256]{1,0:T(1,128)} %items_hbm.1, s32[1,32]{1,0:T(1,128)} %days_hbm.1, s32[1,32,256,256]{3,2,1,0:T(8,128)} %status_hbm.1, f32[32,128]{1,0:T(8,128)} %bitcast.12, f32[32,128]{1,0:T(8,128)} %bitcast.14, f32[32,32]{1,0:T(8,128)} %refs_6_.1), custom_call_target="tpu_custom_call" | custom-call | tf_op jit(solution)/shard_map/step/pallas_call | solution.py:435
  42.8 0.0 copy-done.3
  42.8 0.0 copy-done.9
  42.8 0.0 copy-done.8
  42.8 0.0 copy-done.7
  42.8 0.0 copy-done.6
  42.8 0.0 copy-done.2
  42.8 0.0 copy-done.5
  42.9 0.0 copy-done.4
  42.9 0.0 copy-done.1
  42.9 0.0 copy-start
  42.9 0.8 %copy-done = f32[32,384]{1,0:T(8,128)S(1)} copy-done((f32[32,384]{1,0:T(8,128)S(1)}, f32[32,384]{1,0:T(8,128)}, u32[]{:S(2)}) %copy-start) | copy-done | bytes 49176
  43.7 1.1 %adam.1 = (f32[32,128]{1,0:T(8,128)}, f32[32,128]{1,0:T(8,128)}, f32[32,128]{1,0:T(8,128)}, f32[32,128]{1,0:T(8,128)}, f32[32,128]{1,0:T(8,128)}, /*index=5*/f32...) custom-call(f32[32,384]{1,0:T(8,128)S(1)} %copy-done, f32[32,128]{1,0:T(8,128)S(1)} %bitcast.13, ...), custom_call_target="tpu_custom_call" | custom-call | tf_op jit(solution)/shard_map/adam/pallas_call | solution.py:493
Async XLA Ops:
  0.6 42.1 %copy-start.3 = (f32[32,32]{1,0:T(8,128)S(1)}, f32[32,32]{1,0:T(8,128)}, u32[]{:S(2)}) copy-start(f32[32,32]{1,0:T(8,128)} %refs_6_.1) | copy-start | bytes 12292
  0.7 42.1 %copy-start.9 = (f32[32,32]{1,0:T(8,128)S(1)}, f32[32,32]{1,0:T(8,128)}, u32[]{:S(2)}) copy-start(f32[32,32]{1,0:T(8,128)} %refs_8_.1) | copy-start | bytes 12292
  0.7 42.1 %copy-start.8 = (f32[32,32]{1,0:T(8,128)S(1)}, f32[32,32]{1,0:T(8,128)}, u32[]{:S(2)}) copy-start(f32[32,32]{1,0:T(8,128)} %refs_7_.1) | copy-start | bytes 12292
  0.7 42.1 %copy-start.7 = (f32[128,32]{0,1:T(8,128)S(1)}, f32[128,32]{0,1:T(8,128)}, u32[]{:S(2)}) copy-start(f32[128,32]{0,1:T(8,128)} %param.22) | copy-start | bytes 49156
  0.7 42.1 %copy-start.6 = (f32[128,32]{0,1:T(8,128)S(1)}, f32[128,32]{0,1:T(8,128)}, u32[]{:S(2)}) copy-start(f32[128,32]{0,1:T(8,128)} %param.21) | copy-start | bytes 49156
  0.7 42.1 %copy-start.2 = (f32[128,32]{0,1:T(8,128)S(1)}, f32[128,32]{0,1:T(8,128)}, u32[]{:S(2)}) copy-start(f32[128,32]{0,1:T(8,128)} %param.20) | copy-start | bytes 49156
  0.7 42.1 %copy-start.5 = (f32[128,32]{0,1:T(8,128)S(1)}, f32[128,32]{0,1:T(8,128)}, u32[]{:S(2)}) copy-start(f32[128,32]{0,1:T(8,128)} %param.19) | copy-start | bytes 49156
  0.7 42.1 %copy-start.4 = (f32[128,32]{0,1:T(8,128)S(1)}, f32[128,32]{0,1:T(8,128)}, u32[]{:S(2)}) copy-start(f32[128,32]{0,1:T(8,128)} %param.18) | copy-start | bytes 49156
  0.7 42.1 %copy-start.1 = (f32[128,32]{0,1:T(8,128)S(1)}, f32[128,32]{0,1:T(8,128)}, u32[]{:S(2)}) copy-start(f32[128,32]{0,1:T(8,128)} %param.17) | copy-start | bytes 49156
  42.9 0.8 %copy-start = (f32[32,384]{1,0:T(8,128)S(1)}, f32[32,384]{1,0:T(8,128)}, u32[]{:S(2)}) copy-start(f32[32,384]{1,0:T(8,128)} %step.1.grad_ref) | copy-start | bytes 147460
